TPU v7x, 256 devices: a whole 4x4x8 slice. The times are simulated.
256 devices in a mesh: wall: 16 (over x, z_lo), spec: 16 (over y, z_hi, core).
Axes of the slice: x: 4, y: 4, z: 8 (z_hi: 2, z_lo: 4; z = z_hi * 4 + z_lo), core: 2. Of those that a mesh axis runs over, the one named last changes fastest.
Arguments:
- signal: bfloat16 [4, 2, 512, 32, 10240], P(None, None, 'wall', None, 'spec'), may hold values from -6 to 6
- kx_index: int32 [128], replicated, may hold values from 0 to 5119
- kz_index: int32 [128], replicated, may hold values from 0 to 3
Outputs:
- phi: float32 [2, 128, 512, 512], P(None, 'spec', 'wall')
Inputs may be any that keep to these rules, and one draw needn't show every extreme that they name: `kx_index`: pairs may repeat.
All inputs are finite; a program needn't handle non-finite values.
Results may differ from a plain program's by a relative error of at most 0.0042.
Values sent between devices are 32-bit elements; how exact they have to be, the bound alone decides.
No kernel may reach another device: no remote copies, remote signals or barrier semaphores. Data moves between devices by JAX's collectives and lax.ppermute only.
A program may use at most 64 MiB of HBM per device.

v0:
```python
import math

import jax
import jax.numpy as jnp
from jax import lax
from jax.sharding import PartitionSpec as P

NXW = 10240


def in_blocks(shard, dim, length):
    shape = shard.shape
    parts = shard.reshape(*shape[:dim], length, shape[dim] // length, *shape[dim + 1 :])
    return jnp.moveaxis(parts, dim, 0)


def summed_on_arrival(shard, axis, dim):
    length = lax.axis_size(axis)
    parts = lax.all_to_all(in_blocks(shard, dim, length), axis, 0, 0, tiled=True)
    return jnp.sum(parts, axis=0)


def joined_along(parts, dim):
    parts = jnp.moveaxis(parts, 0, dim)
    shape = parts.shape
    return parts.reshape(*shape[:dim], shape[dim] * shape[dim + 1], *shape[dim + 2 :])


def copy_for_each(shard, axis):
    copies = jnp.broadcast_to(shard, (lax.axis_size(axis), *shard.shape))
    return lax.all_to_all(copies, axis, split_axis=0, concat_axis=0, tiled=True)


def gather_directly(shard, axis, dim):
    return joined_along(copy_for_each(shard, axis), dim)


def tables(kx_values, positions):
    phase = kx_values[:, None] * positions[None, :] % NXW
    angle = 2.0 * math.pi / NXW * phase.astype(jnp.float32)
    factor = float(NXW) ** (-0.5)
    return (
        (jnp.cos(angle) * factor).astype(jnp.bfloat16),
        (jnp.sin(angle) * factor).astype(jnp.bfloat16),
    )


def gram(left, right):
    high = lax.Precision.HIGHEST
    left_re, left_im = (left[:, 0], left[:, 1])
    right_re, right_im = (right[:, 0], right[:, 1])
    snaps = left.shape[3]
    real = (
        jnp.einsum("kys,kzs->kyz", left_re, right_re, precision=high)
        + jnp.einsum("kys,kzs->kyz", left_im, right_im, precision=high)
    ) / snaps
    imag = (
        jnp.einsum("kys,kzs->kyz", left_im, right_re, precision=high)
        - jnp.einsum("kys,kzs->kyz", left_re, right_im, precision=high)
    ) / snaps
    return jnp.stack([real, imag])


def on_device(signal, kx_index, kz_index):
    modes, parts, planes, snaps, width = signal.shape
    flat = signal.reshape(modes, parts, planes * snaps, width)
    positions = lax.axis_index("spec") * width + jnp.arange(width, dtype=jnp.int32)
    local_pairs = kx_index.shape[0] // lax.axis_size("spec")
    cosine, sine = tables(kx_index, positions)
    basis = jnp.stack([cosine, sine])
    grid = jnp.einsum("jcrx,bkx->cbjrk", flat, basis, preferred_element_type=jnp.float32)
    real = grid[0, 0] + grid[1, 1]
    imag = grid[1, 0] - grid[0, 1]
    onehot = (kz_index[None, :] == jnp.arange(modes, dtype=jnp.int32)[:, None]).astype(jnp.float32)
    high = lax.Precision.HIGHEST
    real_pick = jnp.einsum("jrk,jk->kr", real, onehot, precision=high)
    imag_pick = jnp.einsum("jrk,jk->kr", imag, onehot, precision=high)
    local = summed_on_arrival(jnp.stack([real_pick, imag_pick], 1), "spec", 0)
    spectra = local.reshape(local_pairs, 2, planes, snaps)
    return gram(spectra, gather_directly(spectra, "wall", 2))


def solution(mesh):
    return jax.shard_map(
        on_device,
        mesh=mesh,
        in_specs=(P(None, None, "wall", None, "spec"), P(), P()),
        out_specs=P(None, "spec", "wall", None),
        check_vma=False,
    )
```

profile of v0, /device:TPU:6, one launch (start us, length us, event | category | flops | bytes accessed | tf_op | source)
XLA Modules:
  0.0 120.5 jit_solution(16925775208775287407)
XLA Ops:
  0.0 2.2 %multiply_convert_fusion.1 = (bf16[1,128,640]{2,1,0:T(8,128)(2,1)S(1)}, bf16[1,128,640]{2,1,0:T(8,128)(2,1)S(1)}) fusion(s32[640]{0:T(1024)S(1)} %iota_add_fusion, s32[128]{0:T(128)} %param.4), kind=kLoop, calls=%fused_computation.30 | loop fusion | flops 1064960 | bytes 330752 | tf_op jit(solution)/shard_map/convert_element_type | solution.py:43
  2.2 6.2 %convolution_bitcast_fusion = f32[2,2,4,1024,128]{3,4,0,2,1:T(8,128)S(1)} fusion(bf16[4,2,1024,640,1]{3,2,1,0,4:T(8,128)(2,1)} %bitcast.59, bf16[1,128,640]{2,1,0:T(8,128)(2,1)S(1)} %get-tuple-element.8, bf16[1,128,640]{2,1,0:T(8,128)(2,1)S(1)} %get-tuple-element.7), kind=kOutput, calls=%fused_computation | convolution fusion | flops 2685009920 | bytes 19202048 | tf_op jit(solution)/shard_map/jcrx,bkx->cbjrk/dot_general | solution.py:71
  8.5 0.0 copy-start
  8.5 2.3 %fusion.1 = (f32[4,1024,128]{1,2,0:T(8,128)}, f32[4,1024,128]{1,2,0:T(8,128)S(1)}) fusion(f32[2,2,4,1024,128]{3,4,0,2,1:T(8,128)S(1)} %convolution_bitcast_fusion), kind=kLoop, calls=%fused_computation.4 | loop fusion | flops 1048576 | bytes 12582912 | tf_op jit(solution)/shard_map/add | solution.py:72
  10.8 0.0 copy-done
  10.8 0.2 copy.9
  11.0 4.9 %fusion.4 = f32[128,1,1024]{2,1,0:T(1,128)S(1)} fusion(pred[4,128,1]{0,2,1:T(4,128)(4,1)S(1)} %copy.9, f32[4,1024,128]{1,2,0:T(8,128)} %get-tuple-element.5), kind=kOutput, calls=%fused_computation.7 | convolution fusion | flops 6291456 | bytes 2621952 | tf_op jit(solution)/shard_map/jrk,jk->kr/dot_general | solution.py:76
  15.9 3.3 %fusion.2 = f32[128,1,1024]{2,1,0:T(1,128)S(1)} fusion(pred[4,128,1]{0,2,1:T(4,128)(4,1)S(1)} %copy.9, f32[4,1024,128]{1,2,0:T(8,128)S(1)} %get-tuple-element.6), kind=kOutput, calls=%fused_computation.5 | convolution fusion | flops 6291456 | bytes 2621952 | tf_op jit(solution)/shard_map/jrk,jk->kr/dot_general | solution.py:77
  19.2 0.2 copy_bitcast_fusion
  19.4 0.1 pad_maximum_fusion
  19.5 33.7 %all_to_all.10 = f32[16,8,2,1024]{3,1,2,0:T(8,128)S(1)} all-to-all(f32[16,8,2,1024]{3,1,2,0:T(8,128)S(1)} %pad_maximum_fusion), channel_id=1, replica_groups=mesh['wall'=16,'spec'=16] {'spec'}, dimensions={0} | all-to-all | bytes 2097152 | tf_op jit(solution)/shard_map/all_to_all | solution.py:19
  53.3 0.1 reduce_sum.9
  53.3 0.1 reshape.143
  53.5 0.1 copy.5
  53.6 2.5 %broadcast_bitcast_fusion = f32[16,2,8,32,32]{4,3,2,1,0:T(8,128)} fusion(f32[8,2,32,32]{2,3,0,1:T(8,128)S(1)} %copy.5), kind=kLoop, calls=%fused_computation.42 | loop fusion | bytes 1114112
  56.1 3.9 %reshape.150 = f32[16,1,16384]{2,1,0:T(1,128)S(1)} reshape(f32[16,2,8,32,32]{4,3,2,1,0:T(8,128)} %broadcast_bitcast_fusion) | data formatting | bytes 2097152
  60.0 39.3 %all_to_all.11 = f32[16,1,16384]{2,1,0:T(1,128)S(1)} all-to-all(f32[16,1,16384]{2,1,0:T(1,128)S(1)} %reshape.150), channel_id=1, replica_groups=mesh['wall'=16,'spec'=16] {'wall'}, dimensions={0} | all-to-all | bytes 2097152 | tf_op jit(solution)/shard_map/all_to_all | solution.py:31
  99.3 0.5 broadcast.158
  99.8 3.1 %reduce = f32[16,16384]{1,0:T(8,128)S(1)} reduce(f32[16,1,16384]{2,1,0:T(1,128)S(1)} %all_to_all.11, f32[]{:T(128)} %broadcast.158), dimensions={1}, to_apply=%all_to_all.7.reduce_sub_computation | reduce | bytes 2097156 | tf_op jit(solution)/shard_map/all_to_all | solution.py:31
  103.0 2.7 %reshape.151 = f32[16,2,8,32,32]{4,3,2,1,0:T(8,128)} reshape(f32[16,16384]{1,0:T(8,128)S(1)} %reduce) | data formatting | bytes 2097152
  105.7 2.8 %bitcast_bitcast_fusion = f32[8,2,16,32,32]{3,4,0,1,2:T(8,128)S(1)} fusion(f32[16,2,8,32,32]{4,3,2,1,0:T(8,128)} %reshape.151), kind=kLoop, calls=%fused_computation.41 | loop fusion | bytes 2097152 | tf_op jit(solution)/shard_map/transpose | solution.py:24
  108.4 5.2 %copy.6 = f32[8,2,16,32,32]{3,2,4,0,1:T(8,128)} copy(f32[8,2,16,32,32]{3,4,0,1,2:T(8,128)S(1)} %bitcast_bitcast_fusion) | data formatting | bytes 2097152 | tf_op jit(solution)/shard_map/transpose | solution.py:24
  113.6 3.5 %reshape.144 = f32[8,2,512,32]{2,3,0,1:T(8,128)S(1)} reshape(f32[8,2,16,32,32]{3,2,4,0,1:T(8,128)} %copy.6) | data formatting | bytes 2097152 | tf_op jit(solution)/shard_map/reshape | solution.py:26
  117.2 0.6 fusion.11
  117.7 0.6 fusion.10
  118.3 0.6 fusion.9
  118.8 0.6 fusion.7
  119.4 1.1 pad_maximum_fusion.1
  (2 shorter events, 0.0 us)
Async XLA Ops:
  8.5 2.3 %copy-start = (s32[128]{0:T(128)S(1)}, s32[128]{0:T(128)}, u32[]{:S(2)}) copy-start(s32[128]{0:T(128)} %param.5) | copy-start | bytes 1540
where the time goes:
time: 122 us; the launch traced here: 120 us
  blocking collectives  73.1 us (60%)
  local copies, waits for them, and re-layouts  21.7 us (18%)
  matrix products  16.7 us (14%)
  other arithmetic  8.91 us (7%)
    all_to_all x1, blocking collectives, copy_for_each(): return lax.all_to_all(copies, axis, split_axis=0, concat_axis=0, tiled=True)  39.3 us
    all_to_all x1, blocking collectives, summed_on_arrival(): lax.all_to_all(in_blocks(shard, dim, length), axis, 0, 0, tiled=True)  33.7 us
    unnamed x5, local copies, waits for them, and re-layouts  9.05 us
    transpose x2, local copies, waits for them, and re-layouts, joined_along(): parts = jnp.moveaxis(parts, 0, dim)  7.93 us
    dot_general x1, matrix products, on_device(): jnp.einsum('jcrx,bkx->cbjrk', flat, basis, preferred_element_type=jnp.flo...  6.22 us
    dot_general x1, matrix products, on_device(): real_pick = jnp.einsum('jrk,jk->kr', real, onehot, precision=high)  4.92 us
    reshape x1, local copies, waits for them, and re-layouts, joined_along(): parts.reshape(*shape[:dim], shape[dim] * shape[dim + 1], *shape[dim + 2:])  3.54 us
    dot_general x1, matrix products, on_device(): imag_pick = jnp.einsum('jrk,jk->kr', imag, onehot, precision=high)  3.32 us

commit v1 on v0

v1 whole, which is shorter than its diff:
```python
import math

import jax
import jax.numpy as jnp
from jax import lax
from jax.experimental import pallas as pl
from jax.experimental.pallas import tpu as pltpu
from jax.sharding import Mesh
from jax.sharding import PartitionSpec as P

NXW = 10240
QUARTER = NXW // 4
SIN = (1.0, -1.0 / 6, 1.0 / 120, -1.0 / 5040, 1.0 / 362880)
COS = (1.0, -0.5, 1.0 / 24, -1.0 / 720, 1.0 / 40320)
FINE = ("x", "zl", "y", "zh", "core")
WALL, SPEC = FINE[:2], FINE[2:]
VMEM = pl.BlockSpec(memory_space=pltpu.VMEM)
SMEM = pl.BlockSpec(memory_space=pltpu.SMEM)
HBM = pl.BlockSpec(memory_space=pl.ANY)
PARAMS = pltpu.CompilerParams(vmem_limit_bytes=48 * 2**20)


def horner(coefficients, square):
    total = jnp.full_like(square, coefficients[-1])
    for value in coefficients[-2::-1]:
        total = total * square + value
    return total


def basis_columns(kx_row, positions):
    product = positions * kx_row
    quarter = jnp.floor(product.astype(jnp.float32) * (1.0 / QUARTER) + 0.5).astype(jnp.int32)
    angle = (product - quarter * QUARTER).astype(jnp.float32) * (2.0 * math.pi / NXW)
    square = angle * angle
    sine = horner(SIN, square) * angle
    cosine = horner(COS, square)
    swap = (quarter & 1) == 1
    factor = float(NXW) ** -0.5
    first = jnp.where(swap, sine, cosine) * factor
    second = jnp.where(swap, cosine, sine) * factor
    first = jnp.where(((quarter + 1) & 2) == 2, -first, first)
    second = jnp.where((quarter & 2) == 2, -second, second)
    return first.astype(jnp.bfloat16), second.astype(jnp.bfloat16)


def dft_kernel(place, kx_ref, kz_ref, signal, mine, other, held, basis, sems):
    modes, parts, quads, groups, snaps, width = signal.shape
    chunks = sems.shape[0]
    per = groups // chunks
    copies = []
    for t in range(chunks):
        part = pl.ds(t * per, per)
        copy = pltpu.make_async_copy(signal.at[:, :, :, part], held.at[:, :, :, part], sems.at[t])
        copy.start()
        copies.append(copy)
    pairs = kx_ref.shape[1]
    rows = lax.broadcasted_iota(jnp.int32, (width, pairs), 0) + place[0]
    cosine, sine = basis_columns(kx_ref[...], rows)
    basis[:width, :pairs] = cosine
    basis[:width, pairs:] = -sine
    basis[width:, :pairs] = sine
    basis[width:, pairs:] = cosine
    table = basis[...]
    kz = kz_ref[...]
    y, zh, core = place[1], place[2], place[3]
    for t in range(chunks):
        copies[t].wait()
        total = None
        for j in range(modes):
            lines = []
            for g in range(t * per, t * per + per):
                halves = [held[j, c, :, g].reshape(quads * snaps, width) for c in range(parts)]
                lines.append(jnp.concatenate(halves, axis=1))
            lines = jnp.concatenate(lines, axis=0)
            product = jnp.dot(lines, table, preferred_element_type=jnp.float32)
            if total is None:
                total = product
            else:
                total = jnp.where(jnp.concatenate([kz, kz], axis=1) == j, product, total)
        for i in range(per):
            g = t * per + i
            turned = total[i * 128 : (i + 1) * 128].T
            for yy in range(4):
                slot = (yy + 4 - y) & 3
                for zz in range(2):
                    for c in range(parts):
                        at = c * pairs + (yy * 4 + zz * 2) * 8
                        low, high = turned[at : at + 8], turned[at + 8 : at + 16]
                        mine[slot, zz ^ zh, c, g] = jnp.where(core == 0, low, high)
                        other[slot, zz ^ zh, c, g] = jnp.where(core == 0, high, low)


def dft(place, kx_index, kz_index, signal):
    modes, parts, planes, snaps, width = signal.shape
    pairs = kx_index.shape[0]
    view = signal.reshape(modes, parts, 4, planes // 4, snaps, width)
    chunks = 4
    block = jax.ShapeDtypeStruct((4, 2, parts, planes // 4, 8, 128), jnp.float32)
    return pl.pallas_call(
        dft_kernel,
        out_shape=(block, block),
        in_specs=[SMEM, VMEM, VMEM, HBM],
        out_specs=(VMEM, VMEM),
        scratch_shapes=[
            pltpu.VMEM(view.shape, signal.dtype),
            pltpu.VMEM((parts * width, 2 * pairs), jnp.bfloat16),
            pltpu.SemaphoreType.DMA((chunks,)),
        ],
        compiler_params=PARAMS,
        name="dft",
    )(place, kx_index.reshape(1, pairs), kz_index.reshape(1, pairs), view)


def turn_kernel(own_ref, came_ref, out_ref, total):
    total[...] = own_ref[...].reshape(total.shape) + came_ref[...].reshape(total.shape)
    lane = lax.broadcasted_iota(jnp.int32, (8, 128), 1) // 32
    for kk in range(4):
        tiles = []
        for k2 in range(2):
            for c in range(2):
                tiles.append(total[c, pl.ds(2 * kk + k2, 8, stride=8), :])
        for q in range(4):
            row = None
            for j, tile in enumerate(tiles):
                shift = ((j - q) * 32) % 128
                moved = tile if shift == 0 else pltpu.roll(tile, shift, 1)
                row = moved if row is None else jnp.where(lane == j, moved, row)
            out_ref[kk, q * 8 : (q + 1) * 8, :] = row


def turn(own, came):
    return pl.pallas_call(
        turn_kernel,
        out_shape=jax.ShapeDtypeStruct((4, 32, 128), jnp.float32),
        in_specs=[VMEM, VMEM],
        out_specs=VMEM,
        scratch_shapes=[pltpu.VMEM((2, 64, 128), jnp.float32)],
        compiler_params=PARAMS,
        name="turn",
    )(own, came)


def gram_kernel(place, own_ref, *refs):
    blocks, out_ref = refs[:-1], refs[-1]
    x = place[4]
    lane = lax.broadcasted_iota(jnp.int32, (32, 128), 1) // 32
    for kk in range(4):
        own = own_ref[kk] * (1.0 / 32)
        turned = jnp.where(lane % 2 == 0, pltpu.roll(own, 96, 1), -pltpu.roll(own, 32, 1))
        left = []
        for k2 in range(2):
            keep = lane // 2 == k2
            left.append(jnp.where(keep, own, 0.0))
            left.append(jnp.where(keep, turned, 0.0))
        left = jnp.concatenate(left, axis=0).astype(jnp.bfloat16)
        for i, block in enumerate(blocks):
            right = block[:, kk].reshape(128, 128).astype(jnp.bfloat16)
            product = lax.dot_general(
                left, right, (((1,), (1,)), ((), ())), preferred_element_type=jnp.float32
            )
            at = pl.multiple_of(((x + 4 - i) & 3) * 128, 128)
            for k2 in range(2):
                for c in range(2):
                    base = (k2 * 2 + c) * 32
                    out_ref[c, 2 * kk + k2, :, pl.ds(at, 128)] = product[base : base + 32]


def gram(place, own, blocks):
    return pl.pallas_call(
        gram_kernel,
        out_shape=jax.ShapeDtypeStruct((2, 8, 32, 512), jnp.float32),
        in_specs=[SMEM, VMEM] + [VMEM] * len(blocks),
        out_specs=VMEM,
        compiler_params=PARAMS,
        name="gram",
    )(place, own, *blocks)


def shifted(array, axis, by):
    size = lax.axis_size(axis)
    return lax.ppermute(array, axis, [(s, (s + by) % size) for s in range(size)])


def on_device(signal, kx_index, kz_index):
    width = signal.shape[-1]
    y, zh, core = (lax.axis_index(name) for name in SPEC)
    at = lax.axis_index(SPEC) * width
    place = jnp.stack([at, y, zh, core, lax.axis_index("x")]).astype(jnp.int32)
    mine, other = dft(place, kx_index, kz_index, signal)
    summed = mine + shifted(other, "core", 1)
    came = [shifted(summed[i], "y", i) for i in (1, 2, 3)]
    halves = summed[0] + came[0] + came[1] + came[2]
    own = turn(halves[0], shifted(halves[1], "zh", 1))
    column = lax.all_to_all(jnp.broadcast_to(own, (4, *own.shape)), "zl", 0, 0, tiled=True)
    blocks = [column] + [shifted(column, "x", i) for i in (1, 2, 3)]
    return gram(place, own, blocks)


def solution(mesh):
    fine = Mesh(mesh.devices.reshape(4, 4, 4, 2, 2), FINE)
    return jax.shard_map(
        on_device,
        mesh=fine,
        in_specs=(P(None, None, WALL, None, SPEC), P(), P()),
        out_specs=P(None, SPEC, WALL, None),
        check_vma=False,
    )
```

time: 122 us -> 58.6 us (0.48)
  the two profiles are of different devices: /device:TPU:6 before, /device:TPU:225 now
where the time goes in v1:
time: 58.6 us; the launch traced here: 58.4 us
  waiting for transfers between devices  28 us (48%)
  blocking collectives  10.6 us (18%)
  starting transfers between devices  10.1 us (17%)
  Pallas kernels  8.1 us (14%)
  local copies, waits for them, and re-layouts  1.45 us (2%)
    ppermute x8, waiting for transfers between devices, shifted(): lax.ppermute(array, axis, [(s, (s + by) % size) for s in range(size)])  28 us
    all_to_all x1, blocking collectives, on_device(): lax.all_to_all(jnp.broadcast_to(own, (4, *own.shape)), 'zl', 0, 0, tiled=...  10.6 us
    ppermute x8, starting transfers between devices, shifted(): lax.ppermute(array, axis, [(s, (s + by) % size) for s in range(size)])  10.1 us
    pallas_call x1, Pallas kernels, dft(): pl.pallas_call(dft_kernel, out_shape=(block, block), in_specs=[SMEM, VMEM...  5.97 us
    pallas_call x1, Pallas kernels, gram(): pl.pallas_call(gram_kernel, out_shape=jax.ShapeDtypeStruct((2, 8, 32, 512...  2 us
    unnamed x4, local copies, waits for them, and re-layouts  1.31 us
  transfers between devices with their start and end apart: 8, of which 7 were waited for; matrix products, arithmetic and copies ran while one was open for 0% of the time, Pallas kernels for 0%

profile of v1, /device:TPU:225, one launch (start us, length us, event | category | flops | bytes accessed | tf_op | source)
XLA Modules:
  0.0 58.4 jit_solution(6540297782661809147)
XLA Ops:
  0.0 0.1 stack.23.place
  0.1 0.0 copy-start
  0.1 0.7 %copy-done = s32[128]{0:T(128)S(1)} copy-done((s32[128]{0:T(128)S(1)}, s32[128]{0:T(128)}, u32[]{:S(2)}) %copy-start) | copy-done | bytes 536
  0.7 0.0 copy-start.1
  0.7 0.7 %copy-done.1 = s32[128]{0:T(128)S(1)} copy-done((s32[128]{0:T(128)S(1)}, s32[128]{0:T(128)}, u32[]{:S(2)}) %copy-start.1) | copy-done | bytes 536
  1.4 6.0 %dft.1 = (f32[4,2,2,8,8,128]{5,4,3,2,1,0:T(8,128)S(1)}, f32[4,2,2,8,8,128]{5,4,3,2,1,0:T(8,128)S(1)}) custom-call(s32[5]{0:T(128)S(1)} %stack.23.place, s32[1,128]{1,0:T(1,128)S(1)} %bitcast.26, s32[1,128]{1,0:T(1,128)S(1)} %bitcast.27, bf16[4,2,4,8,32,640]{5,4,3,2,1,0:T(8,128)(2,1)} %bitcast.28), custom_call_target="tpu_custom_call" | custom-call | tf_op jit(solution)/shard_map/dft/pallas_call | solution.py:99
  7.4 0.8 %collective-permute-start = (f32[4,2,2,8,8,128]{5,4,3,2,1,0:T(8,128)S(1)}, f32[4,2,2,8,8,128]{5,4,3,2,1,0:T(8,128)S(1)}, u32[]{:S(2)}, u32[]{:S(2)}) collective-permute-start(f32[4,2,2,8,8,128]{5,4,3,2,1,0:T(8,128)S(1)} %get-tuple-element.8), channel_id=1, source_target_pairs={{0,1},{1,0},{2,3},{3,2},{4,5},{5,4},{6,7},{7,6},{8,9},{9,8},{10,11... | collective-permute-start | bytes 1572872 | tf_op jit(solution)/shard_map/ppermute | solution.py:181
  8.1 1.5 %collective-permute-done = f32[4,2,2,8,8,128]{5,4,3,2,1,0:T(8,128)S(1)} collective-permute-done((f32[4,2,2,8,8,128]{5,4,3,2,1,0:T(8,128)S(1)}, f32[4,2,2,8,8,128]{5,4,3,2,1,0:T(8,128)S(1)}, u32[]{:S(2)}, u32[]{:S(2)}) %collective-permute-start) | collective-permute-done | bytes 524320 | tf_op jit(solution)/shard_map/ppermute | solution.py:181
  9.7 0.1 add.20
  9.8 1.4 %collective-permute-start.1 = (f32[2,2,8,8,128]{4,3,2,1,0:T(8,128)S(1)}, f32[2,2,8,8,128]{4,3,2,1,0:T(8,128)S(1)}, u32[]{:S(2)}, u32[]{:S(2)}) collective-permute-start(f32[2,2,8,8,128]{4,3,2,1,0:T(8,128)S(1)} %get-tuple-element.9), channel_id=1, source_target_pairs={{0,4},{4,8},{8,12},{12,0},{1,5},{5,9},{9,13},{13,1},{2,6},{6,10},{... | collective-permute-start | bytes 393224 | tf_op jit(solution)/shard_map/ppermute | solution.py:181
  11.1 1.5 %collective-permute-start.3 = (f32[2,2,8,8,128]{4,3,2,1,0:T(8,128)S(1)}, f32[2,2,8,8,128]{4,3,2,1,0:T(8,128)S(1)}, u32[]{:S(2)}, u32[]{:S(2)}) collective-permute-start(f32[2,2,8,8,128]{4,3,2,1,0:T(8,128)S(1)} %get-tuple-element.10), channel_id=1, source_target_pairs={{0,12},{4,0},{8,4},{12,8},{1,13},{5,1},{9,5},{13,9},{2,14},{6,2},{... | collective-permute-start | bytes 393224 | tf_op jit(solution)/shard_map/ppermute | solution.py:181
  12.7 1.6 %collective-permute-start.2 = (f32[2,2,8,8,128]{4,3,2,1,0:T(8,128)S(1)}, f32[2,2,8,8,128]{4,3,2,1,0:T(8,128)S(1)}, u32[]{:S(2)}, u32[]{:S(2)}) collective-permute-start(f32[2,2,8,8,128]{4,3,2,1,0:T(8,128)S(1)} %get-tuple-element.11), channel_id=1, source_target_pairs={{0,8},{4,12},{8,0},{12,4},{1,9},{5,13},{9,1},{13,5},{2,10},{6,14},... | collective-permute-start | bytes 393224 | tf_op jit(solution)/shard_map/ppermute | solution.py:181
  14.2 1.7 %collective-permute-done.1 = f32[2,2,8,8,128]{4,3,2,1,0:T(8,128)S(1)} collective-permute-done((f32[2,2,8,8,128]{4,3,2,1,0:T(8,128)S(1)}, f32[2,2,8,8,128]{4,3,2,1,0:T(8,128)S(1)}, u32[]{:S(2)}, u32[]{:S(2)}) %collective-permute-start.1) | collective-permute-done | bytes 131104 | tf_op jit(solution)/shard_map/ppermute | solution.py:181
  15.9 0.0 collective-permute-done.3
  15.9 3.9 %collective-permute-done.2 = f32[2,2,8,8,128]{4,3,2,1,0:T(8,128)S(1)} collective-permute-done((f32[2,2,8,8,128]{4,3,2,1,0:T(8,128)S(1)}, f32[2,2,8,8,128]{4,3,2,1,0:T(8,128)S(1)}, u32[]{:S(2)}, u32[]{:S(2)}) %collective-permute-start.2) | collective-permute-done | bytes 131104 | tf_op jit(solution)/shard_map/ppermute | solution.py:181
  19.9 1.2 %collective-permute-start.4 = (f32[2,8,8,128]{3,2,1,0:T(8,128)S(1)}, f32[2,8,8,128]{3,2,1,0:T(8,128)S(1)}, u32[]{:S(2)}, u32[]{:S(2)}) collective-permute-start(f32[2,8,8,128]{3,2,1,0:T(8,128)S(1)} %get-tuple-element.12), channel_id=1, source_target_pairs={{0,2},{2,0},{1,3},{3,1},{4,6},{6,4},{5,7},{7,5},{8,10},{10,8},{9,1... | collective-permute-start | bytes 196616 | tf_op jit(solution)/shard_map/ppermute | solution.py:181
  21.1 6.7 %collective-permute-done.4.came_ref = f32[2,8,8,128]{3,2,1,0:T(8,128)S(1)} collective-permute-done((f32[2,8,8,128]{3,2,1,0:T(8,128)S(1)}, f32[2,8,8,128]{3,2,1,0:T(8,128)S(1)}, u32[]{:S(2)}, u32[]{:S(2)}) %collective-permute-start.4) | collective-permute-done | bytes 65568 | tf_op jit(solution)/shard_map/ppermute | solution.py:181
  27.8 0.1 turn.1.own_ref
  28.0 10.6 %all_to_all.5.refs_0_ = f32[4,4,32,128]{3,2,1,0:T(8,128)S(1)} all-to-all(f32[4,4,32,128]{3,2,1,0:T(8,128)S(1)} %broadcast_in_dim.3), channel_id=1, replica_groups=mesh['x'=4,'zl'=4,'y'=4,'zh'=2,'core'=2] {'zl'}, dimensions={0} | all-to-all | bytes 524288 | tf_op jit(solution)/shard_map/all_to_all | solution.py:194
  38.6 2.5 %collective-permute-start.7 = (f32[4,4,32,128]{3,2,1,0:T(8,128)S(1)}, f32[4,4,32,128]{3,2,1,0:T(8,128)S(1)}, u32[]{:S(2)}, u32[]{:S(2)}) collective-permute-start(f32[4,4,32,128]{3,2,1,0:T(8,128)S(1)} %all_to_all.5.refs_0_), channel_id=1, source_target_pairs={{0,192},{64,0},{128,64},{192,128},{1,193},{65,1},{129,65},{193,129... | collective-permute-start | bytes 786440 | tf_op jit(solution)/shard_map/ppermute | solution.py:181
  41.1 0.5 collective-permute-start.6
  41.6 0.6 %collective-permute-start.5 = (f32[4,4,32,128]{3,2,1,0:T(8,128)S(1)}, f32[4,4,32,128]{3,2,1,0:T(8,128)S(1)}, u32[]{:S(2)}, u32[]{:S(2)}) collective-permute-start(f32[4,4,32,128]{3,2,1,0:T(8,128)S(1)} %all_to_all.5.refs_0_), channel_id=1, source_target_pairs={{0,64},{64,128},{128,192},{192,0},{1,65},{65,129},{129,193},{193,1... | collective-permute-start | bytes 786440 | tf_op jit(solution)/shard_map/ppermute | solution.py:181
  42.2 3.8 %collective-permute-done.7.refs_3_ = f32[4,4,32,128]{3,2,1,0:T(8,128)S(1)} collective-permute-done((f32[4,4,32,128]{3,2,1,0:T(8,128)S(1)}, f32[4,4,32,128]{3,2,1,0:T(8,128)S(1)}, u32[]{:S(2)}, u32[]{:S(2)}) %collective-permute-start.7) | collective-permute-done | bytes 262176 | tf_op jit(solution)/shard_map/ppermute | solution.py:181
  46.0 2.7 %collective-permute-done.6.refs_2_ = f32[4,4,32,128]{3,2,1,0:T(8,128)S(1)} collective-permute-done((f32[4,4,32,128]{3,2,1,0:T(8,128)S(1)}, f32[4,4,32,128]{3,2,1,0:T(8,128)S(1)}, u32[]{:S(2)}, u32[]{:S(2)}) %collective-permute-start.6) | collective-permute-done | bytes 262176 | tf_op jit(solution)/shard_map/ppermute | solution.py:181
  48.7 7.7 %collective-permute-done.5.refs_1_ = f32[4,4,32,128]{3,2,1,0:T(8,128)S(1)} collective-permute-done((f32[4,4,32,128]{3,2,1,0:T(8,128)S(1)}, f32[4,4,32,128]{3,2,1,0:T(8,128)S(1)}, u32[]{:S(2)}, u32[]{:S(2)}) %collective-permute-start.5) | collective-permute-done | bytes 262176 | tf_op jit(solution)/shard_map/ppermute | solution.py:181
  56.4 2.0 %gram.1 = f32[2,8,32,512]{3,2,1,0:T(8,128)} custom-call(s32[5]{0:T(128)S(1)} %stack.23.place, f32[4,32,128]{2,1,0:T(8,128)S(1)} %turn.1.own_ref, f32[4,4,32,128]{3,2,1,0:T(8,128)S(1)} %all_to_all.5.refs_0_, f32[4,4,32,128]{3,2,1,0:T(8,128)S(1)} %collective-permute-done.5.refs_1_, f32[4,4,32,128]{3,2,1,0:T(8,128)S(1)} %collective-permute-done.6.refs_2_, ...), custom_call_target="tpu_custom_call" | custom-call | tf_op jit(solution)/shard_map/gram/pallas_call | solution.py:169
  (4 shorter events, 0.1 us)
Async XLA Ops:
  0.1 0.7 %copy-start = (s32[128]{0:T(128)S(1)}, s32[128]{0:T(128)}, u32[]{:S(2)}) copy-start(s32[128]{0:T(128)} %param.4) | copy-start | bytes 1540
  0.7 0.7 %copy-start.1 = (s32[128]{0:T(128)S(1)}, s32[128]{0:T(128)}, u32[]{:S(2)}) copy-start(s32[128]{0:T(128)} %param.5) | copy-start | bytes 1540
  7.4 2.3 %collective-permute-start = (f32[4,2,2,8,8,128]{5,4,3,2,1,0:T(8,128)S(1)}, f32[4,2,2,8,8,128]{5,4,3,2,1,0:T(8,128)S(1)}, u32[]{:S(2)}, u32[]{:S(2)}) collective-permute-start(f32[4,2,2,8,8,128]{5,4,3,2,1,0:T(8,128)S(1)} %get-tuple-element.8), channel_id=1, source_target_pairs={{0,1},{1,0},{2,3},{3,2},{4,5},{5,4},{6,7},{7,6},{8,9},{9,8},{10,11... | collective-permute-start | bytes 1572872 | tf_op jit(solution)/shard_map/ppermute | solution.py:181
  9.8 6.1 %collective-permute-start.1 = (f32[2,2,8,8,128]{4,3,2,1,0:T(8,128)S(1)}, f32[2,2,8,8,128]{4,3,2,1,0:T(8,128)S(1)}, u32[]{:S(2)}, u32[]{:S(2)}) collective-permute-start(f32[2,2,8,8,128]{4,3,2,1,0:T(8,128)S(1)} %get-tuple-element.9), channel_id=1, source_target_pairs={{0,4},{4,8},{8,12},{12,0},{1,5},{5,9},{9,13},{13,1},{2,6},{6,10},{... | collective-permute-start | bytes 393224 | tf_op jit(solution)/shard_map/ppermute | solution.py:181
  11.1 4.8 %collective-permute-start.3 = (f32[2,2,8,8,128]{4,3,2,1,0:T(8,128)S(1)}, f32[2,2,8,8,128]{4,3,2,1,0:T(8,128)S(1)}, u32[]{:S(2)}, u32[]{:S(2)}) collective-permute-start(f32[2,2,8,8,128]{4,3,2,1,0:T(8,128)S(1)} %get-tuple-element.10), channel_id=1, source_target_pairs={{0,12},{4,0},{8,4},{12,8},{1,13},{5,1},{9,5},{13,9},{2,14},{6,2},{... | collective-permute-start | bytes 393224 | tf_op jit(solution)/shard_map/ppermute | solution.py:181
  12.7 7.1 %collective-permute-start.2 = (f32[2,2,8,8,128]{4,3,2,1,0:T(8,128)S(1)}, f32[2,2,8,8,128]{4,3,2,1,0:T(8,128)S(1)}, u32[]{:S(2)}, u32[]{:S(2)}) collective-permute-start(f32[2,2,8,8,128]{4,3,2,1,0:T(8,128)S(1)} %get-tuple-element.11), channel_id=1, source_target_pairs={{0,8},{4,12},{8,0},{12,4},{1,9},{5,13},{9,1},{13,5},{2,10},{6,14},... | collective-permute-start | bytes 393224 | tf_op jit(solution)/shard_map/ppermute | solution.py:181
  19.9 7.9 %collective-permute-start.4 = (f32[2,8,8,128]{3,2,1,0:T(8,128)S(1)}, f32[2,8,8,128]{3,2,1,0:T(8,128)S(1)}, u32[]{:S(2)}, u32[]{:S(2)}) collective-permute-start(f32[2,8,8,128]{3,2,1,0:T(8,128)S(1)} %get-tuple-element.12), channel_id=1, source_target_pairs={{0,2},{2,0},{1,3},{3,1},{4,6},{6,4},{5,7},{7,5},{8,10},{10,8},{9,1... | collective-permute-start | bytes 196616 | tf_op jit(solution)/shard_map/ppermute | solution.py:181
  38.6 7.4 %collective-permute-start.7 = (f32[4,4,32,128]{3,2,1,0:T(8,128)S(1)}, f32[4,4,32,128]{3,2,1,0:T(8,128)S(1)}, u32[]{:S(2)}, u32[]{:S(2)}) collective-permute-start(f32[4,4,32,128]{3,2,1,0:T(8,128)S(1)} %all_to_all.5.refs_0_), channel_id=1, source_target_pairs={{0,192},{64,0},{128,64},{192,128},{1,193},{65,1},{129,65},{193,129... | collective-permute-start | bytes 786440 | tf_op jit(solution)/shard_map/ppermute | solution.py:181
  41.1 7.7 %collective-permute-start.6 = (f32[4,4,32,128]{3,2,1,0:T(8,128)S(1)}, f32[4,4,32,128]{3,2,1,0:T(8,128)S(1)}, u32[]{:S(2)}, u32[]{:S(2)}) collective-permute-start(f32[4,4,32,128]{3,2,1,0:T(8,128)S(1)} %all_to_all.5.refs_0_), channel_id=1, source_target_pairs={{0,128},{64,192},{128,0},{192,64},{1,129},{65,193},{129,1},{193,65... | collective-permute-start | bytes 786440 | tf_op jit(solution)/shard_map/ppermute | solution.py:181
  41.6 14.8 %collective-permute-start.5 = (f32[4,4,32,128]{3,2,1,0:T(8,128)S(1)}, f32[4,4,32,128]{3,2,1,0:T(8,128)S(1)}, u32[]{:S(2)}, u32[]{:S(2)}) collective-permute-start(f32[4,4,32,128]{3,2,1,0:T(8,128)S(1)} %all_to_all.5.refs_0_), channel_id=1, source_target_pairs={{0,64},{64,128},{128,192},{192,0},{1,65},{65,129},{129,193},{193,1... | collective-permute-start | bytes 786440 | tf_op jit(solution)/shard_map/ppermute | solution.py:181

commit v2 on v1

v2 whole, which is shorter than its diff:
```python
import functools
import math

import jax
import jax.numpy as jnp
from jax import lax
from jax.experimental import pallas as pl
from jax.experimental.pallas import tpu as pltpu
from jax.sharding import Mesh
from jax.sharding import PartitionSpec as P

NXW = 10240
QUARTER = NXW // 4
SIN = (1.0, -1.0 / 6, 1.0 / 120, -1.0 / 5040, 1.0 / 362880)
COS = (1.0, -0.5, 1.0 / 24, -1.0 / 720, 1.0 / 40320)
FINE = ("x", "zl", "y", "zh", "core")
WALL, SPEC = FINE[:2], FINE[2:]
VMEM = pl.BlockSpec(memory_space=pltpu.VMEM)
SMEM = pl.BlockSpec(memory_space=pltpu.SMEM)
HBM = pl.BlockSpec(memory_space=pl.ANY)
FAR = pl.BlockSpec(memory_space=pltpu.HBM)
PARAMS = pltpu.CompilerParams(vmem_limit_bytes=48 * 2**20)


def horner(coefficients, square):
    total = jnp.full_like(square, coefficients[-1])
    for value in coefficients[-2::-1]:
        total = total * square + value
    return total


def basis_columns(kx_row, positions):
    product = positions * kx_row
    quarter = jnp.floor(product.astype(jnp.float32) * (1.0 / QUARTER) + 0.5).astype(jnp.int32)
    angle = (product - quarter * QUARTER).astype(jnp.float32) * (2.0 * math.pi / NXW)
    square = angle * angle
    sine = horner(SIN, square) * angle
    cosine = horner(COS, square)
    swap = (quarter & 1) == 1
    factor = float(NXW) ** -0.5
    first = jnp.where(swap, sine, cosine) * factor
    second = jnp.where(swap, cosine, sine) * factor
    first = jnp.where(((quarter + 1) & 2) == 2, -first, first)
    second = jnp.where((quarter & 2) == 2, -second, second)
    return first.astype(jnp.bfloat16), second.astype(jnp.bfloat16)


CHUNKS = (2, 2, 2, 2)


def dft_kernel(place, kx_hbm, kz_hbm, signal, mine, other, held, basis, kx_ref, kz_ref, sems):
    modes, parts, quads, groups, snaps, width = signal.shape
    pairs = kx_ref.shape[1]
    index = [
        pltpu.make_async_copy(kx_hbm, kx_ref, sems.at[len(CHUNKS)]),
        pltpu.make_async_copy(kz_hbm, kz_ref, sems.at[len(CHUNKS) + 1]),
    ]
    for copy in index:
        copy.start()
    copies, first = [], 0
    for t, size in enumerate(CHUNKS):
        part = pl.ds(first, size)
        copies.append(pltpu.make_async_copy(signal.at[:, :, :, part], held.at[:, :, :, part], sems.at[t]))
        copies[t].start()
        first += size
    for copy in index:
        copy.wait()
    rows = lax.broadcasted_iota(jnp.int32, (width, pairs), 0) + place[0]
    cosine, sine = basis_columns(kx_ref[...], rows)
    basis[:width, :pairs] = cosine
    basis[:width, pairs:] = -sine
    basis[width:, :pairs] = sine
    basis[width:, pairs:] = cosine
    kz = jnp.concatenate([kz_ref[...], kz_ref[...]], axis=1)
    y, zh, core = place[1], place[2], place[3]
    first = 0
    for t, size in enumerate(CHUNKS):
        copies[t].wait()
        total = None
        for j in range(modes):
            lines = []
            for g in range(first, first + size):
                halves = [held[j, c, :, g].reshape(quads * snaps, width) for c in range(parts)]
                lines.append(jnp.concatenate(halves, axis=1))
            lines = jnp.concatenate(lines, axis=0)
            product = jnp.dot(lines, basis[...], preferred_element_type=jnp.float32)
            total = product if total is None else jnp.where(kz == j, product, total)
        for i in range(size):
            turned = total[i * 128 : (i + 1) * 128].T
            for yy in range(4):
                slot = (yy + 4 - y) & 3
                for zz in range(2):
                    for c in range(parts):
                        at = c * pairs + (yy * 4 + zz * 2) * 8
                        low, high = turned[at : at + 8], turned[at + 8 : at + 16]
                        mine[slot, zz ^ zh, c, first + i] = jnp.where(core == 0, low, high)
                        other[slot, zz ^ zh, c, first + i] = jnp.where(core == 0, high, low)
        first += size


def dft(place, kx_index, kz_index, signal):
    modes, parts, planes, snaps, width = signal.shape
    pairs = kx_index.shape[0]
    view = signal.reshape(modes, parts, 4, planes // 4, snaps, width)
    block = jax.ShapeDtypeStruct((4, 2, parts, planes // 4, 8, 128), jnp.float32)
    return pl.pallas_call(
        dft_kernel,
        out_shape=(block, block),
        in_specs=[SMEM, FAR, FAR, HBM],
        out_specs=(VMEM, VMEM),
        scratch_shapes=[
            pltpu.VMEM(view.shape, signal.dtype),
            pltpu.VMEM((parts * width, 2 * pairs), jnp.bfloat16),
            pltpu.VMEM((1, pairs), jnp.int32),
            pltpu.VMEM((1, pairs), jnp.int32),
            pltpu.SemaphoreType.DMA((len(CHUNKS) + 2,)),
        ],
        compiler_params=PARAMS,
        name="dft",
    )(
        place,
        pltpu.with_memory_space_constraint(kx_index.reshape(1, pairs), pltpu.HBM),
        pltpu.with_memory_space_constraint(kz_index.reshape(1, pairs), pltpu.HBM),
        view,
    )


def turn_kernel(own_ref, came_ref, out_ref, total):
    total[...] = own_ref[...].reshape(total.shape) + came_ref[...].reshape(total.shape)
    lane = lax.broadcasted_iota(jnp.int32, (8, 128), 1) // 32
    for kk in range(4):
        tiles = []
        for k2 in range(2):
            for c in range(2):
                tiles.append(total[c, pl.ds(2 * kk + k2, 8, stride=8), :])
        for q in range(4):
            row = None
            for j, tile in enumerate(tiles):
                shift = ((j - q) * 32) % 128
                moved = tile if shift == 0 else pltpu.roll(tile, shift, 1)
                row = moved if row is None else jnp.where(lane == j, moved, row)
            out_ref[kk, q * 8 : (q + 1) * 8, :] = row


def turn(own, came):
    return pl.pallas_call(
        turn_kernel,
        out_shape=jax.ShapeDtypeStruct((4, 32, 128), jnp.float32),
        in_specs=[VMEM, VMEM],
        out_specs=VMEM,
        scratch_shapes=[pltpu.VMEM((2, 64, 128), jnp.float32)],
        compiler_params=PARAMS,
        name="turn",
    )(own, came)


def against(left, right):
    return lax.dot_general(left, right, (((1,), (1,)), ((), ())), preferred_element_type=jnp.float32)


def gram_kernel(spots, place, own_ref, *refs):
    blocks, (out_hbm, right, out, sems) = refs[:-4], refs[-4:]
    x, zl = place[4], place[5]
    lane = lax.broadcasted_iota(jnp.int32, (32, 128), 1) // 32
    copies = []
    for kk in range(4):
        for block, group in zip(blocks, spots):
            for n, (i, j) in enumerate(group):
                at = pl.multiple_of(((x ^ i) * 4 + (zl ^ j)) * 32, 32)
                right[kk, pl.ds(at, 32), :] = block[n, kk].astype(jnp.bfloat16)
        own = own_ref[kk] * (1.0 / 32)
        turned = jnp.where(lane % 2 == 0, pltpu.roll(own, 96, 1), -pltpu.roll(own, 32, 1))
        left = []
        for k2 in range(2):
            keep = lane // 2 == k2
            left.append(jnp.where(keep, own, 0.0))
            left.append(jnp.where(keep, turned, 0.0))
        whole = jnp.concatenate(left, axis=0)
        high = whole.astype(jnp.bfloat16)
        low = (whole - high.astype(jnp.float32)).astype(jnp.bfloat16)
        product = against(jnp.concatenate([high, low], axis=1), jnp.concatenate([right[kk], right[kk]], axis=1))
        for k2 in range(2):
            for c in range(2):
                base = (k2 * 2 + c) * 32
                out[c, 2 * kk + k2] = product[base : base + 32]
        part = pl.ds(2 * kk, 2)
        copies.append(pltpu.make_async_copy(out.at[:, part], out_hbm.at[:, part], sems.at[kk]))
        copies[kk].start()
    for copy in copies:
        copy.wait()


def gram(place, own, blocks, spots):
    shape = (2, 8, 32, 512)
    return pl.pallas_call(
        functools.partial(gram_kernel, spots),
        out_shape=jax.ShapeDtypeStruct(shape, jnp.float32),
        in_specs=[SMEM, VMEM] + [VMEM] * len(blocks),
        out_specs=HBM,
        scratch_shapes=[
            pltpu.VMEM((4, 512, 128), jnp.bfloat16),
            pltpu.VMEM(shape, jnp.float32),
            pltpu.SemaphoreType.DMA((4,)),
        ],
        compiler_params=PARAMS,
        name="gram",
    )(place, own, *blocks)


def shifted(array, axis, by):
    size = lax.axis_size(axis)
    return lax.ppermute(array, axis, [(s, (s + by) % size) for s in range(size)])


def swapped(array, axis, by):
    return lax.ppermute(array, axis, [(s, s ^ by) for s in range(lax.axis_size(axis))])


def gathered(own):
    z3, z2 = (swapped(own, "zl", j) for j in (3, 2))
    x2, x1, x3 = (swapped(own, "x", i) for i in (2, 1, 3))
    blocks = [jnp.stack([own, x1, x2, x3, z2, z3])]
    spots = [[(0, 0), (1, 0), (2, 0), (3, 0), (0, 2), (0, 3)]]
    blocks.append(swapped(blocks[0][:4], "zl", 1))
    spots.append([(i, 1) for i in range(4)])
    for i in (2, 1, 3):
        blocks.append(swapped(jnp.stack([z2, z3]), "x", i))
        spots.append([(i, 2), (i, 3)])
    return blocks, spots


def on_device(signal, kx_index, kz_index):
    width = signal.shape[-1]
    y, zh, core = (lax.axis_index(name) for name in SPEC)
    at = lax.axis_index(SPEC) * width
    place = jnp.stack([at, y, zh, core, lax.axis_index("x"), lax.axis_index("zl")]).astype(jnp.int32)
    mine, other = dft(place, kx_index, kz_index, signal)
    summed = mine + shifted(other, "core", 1)
    came = [shifted(summed[i], "y", i) for i in (2, 1, 3)]
    halves = summed[0] + came[0] + came[1] + came[2]
    own = turn(halves[0], shifted(halves[1], "zh", 1))
    return gram(place, own, *gathered(own))


def solution(mesh):
    fine = Mesh(mesh.devices.reshape(4, 4, 4, 2, 2), FINE)
    return jax.shard_map(
        on_device,
        mesh=fine,
        in_specs=(P(None, None, WALL, None, SPEC), P(), P()),
        out_specs=P(None, SPEC, WALL, None),
        check_vma=False,
    )
```

time: 58.6 us -> 50.4 us (0.86)
  the two profiles are of different devices: /device:TPU:225 before, /device:TPU:6 now
where the time goes in v2:
time: 50.4 us
  starting transfers between devices  25 us (50%)
  waiting for transfers between devices  17 us (34%)
  Pallas kernels  7.96 us (16%)
    ppermute x5, starting transfers between devices, shifted(): lax.ppermute(array, axis, [(s, (s + by) % size) for s in range(size)])  12.7 us
    ppermute x9, starting transfers between devices, swapped(): lax.ppermute(array, axis, [(s, s ^ by) for s in range(lax.axis_size(axis))])  12.3 us
    ppermute x5, waiting for transfers between devices, shifted(): lax.ppermute(array, axis, [(s, (s + by) % size) for s in range(size)])  9.49 us
    ppermute x9, waiting for transfers between devices, swapped(): lax.ppermute(array, axis, [(s, s ^ by) for s in range(lax.axis_size(axis))])  7.5 us
    pallas_call x1, Pallas kernels, dft(): pl.pallas_call(dft_kernel, out_shape=(block, block), in_specs=[SMEM, FAR,...  6.02 us
    pallas_call x1, Pallas kernels, gram(): pl.pallas_call(functools.partial(gram_kernel, spots), out_shape=jax.Shape...  1.82 us
  transfers between devices with their start and end apart: 14, of which 9 were waited for; matrix products, arithmetic and copies ran while one was open for 0% of the time, Pallas kernels for 0%

profile of v2, /device:TPU:6, one launch (start us, length us, event | category | flops | bytes accessed | tf_op | source)
XLA Modules:
  0.0 50.4 jit_solution(3671793466657494212)
XLA Ops:
  0.0 0.1 stack.61.place
  0.1 6.0 %dft.1 = (f32[4,2,2,8,8,128]{5,4,3,2,1,0:T(8,128)S(1)}, f32[4,2,2,8,8,128]{5,4,3,2,1,0:T(8,128)S(1)}) custom-call(s32[6]{0:T(128)S(1)} %stack.61.place, s32[1,128]{1,0:T(1,128)} %bitcast.46, s32[1,128]{1,0:T(1,128)} %bitcast.47, bf16[4,2,4,8,32,640]{5,4,3,2,1,0:T(8,128)(2,1)} %bitcast.40), custom_call_target="tpu_custom_call" | custom-call | tf_op jit(solution)/shard_map/dft/pallas_call | solution.py:106
  6.1 0.1 collective-permute-start
  6.2 1.9 %collective-permute-done = f32[4,2,2,8,8,128]{5,4,3,2,1,0:T(8,128)S(1)} collective-permute-done((f32[4,2,2,8,8,128]{5,4,3,2,1,0:T(8,128)S(1)}, f32[4,2,2,8,8,128]{5,4,3,2,1,0:T(8,128)S(1)}, u32[]{:S(2)}, u32[]{:S(2)}) %collective-permute-start) | collective-permute-done | bytes 524320 | tf_op jit(solution)/shard_map/ppermute | solution.py:212
  8.1 0.1 add.20
  8.2 3.3 %collective-permute-start.1 = (f32[2,2,8,8,128]{4,3,2,1,0:T(8,128)S(1)}, f32[2,2,8,8,128]{4,3,2,1,0:T(8,128)S(1)}, u32[]{:S(2)}, u32[]{:S(2)}) collective-permute-start(f32[2,2,8,8,128]{4,3,2,1,0:T(8,128)S(1)} %get-tuple-element.9), channel_id=1, source_target_pairs={{0,8},{4,12},{8,0},{12,4},{1,9},{5,13},{9,1},{13,5},{2,10},{6,14},... | collective-permute-start | bytes 393224 | tf_op jit(solution)/shard_map/ppermute | solution.py:212
  11.5 1.1 %collective-permute-start.3 = (f32[2,2,8,8,128]{4,3,2,1,0:T(8,128)S(1)}, f32[2,2,8,8,128]{4,3,2,1,0:T(8,128)S(1)}, u32[]{:S(2)}, u32[]{:S(2)}) collective-permute-start(f32[2,2,8,8,128]{4,3,2,1,0:T(8,128)S(1)} %get-tuple-element.10), channel_id=1, source_target_pairs={{0,12},{4,0},{8,4},{12,8},{1,13},{5,1},{9,5},{13,9},{2,14},{6,2},{... | collective-permute-start | bytes 393224 | tf_op jit(solution)/shard_map/ppermute | solution.py:212
  12.5 1.0 %collective-permute-start.2 = (f32[2,2,8,8,128]{4,3,2,1,0:T(8,128)S(1)}, f32[2,2,8,8,128]{4,3,2,1,0:T(8,128)S(1)}, u32[]{:S(2)}, u32[]{:S(2)}) collective-permute-start(f32[2,2,8,8,128]{4,3,2,1,0:T(8,128)S(1)} %get-tuple-element.11), channel_id=1, source_target_pairs={{0,4},{4,8},{8,12},{12,0},{1,5},{5,9},{9,13},{13,1},{2,6},{6,10},{... | collective-permute-start | bytes 393224 | tf_op jit(solution)/shard_map/ppermute | solution.py:212
  13.5 2.5 %collective-permute-done.1 = f32[2,2,8,8,128]{4,3,2,1,0:T(8,128)S(1)} collective-permute-done((f32[2,2,8,8,128]{4,3,2,1,0:T(8,128)S(1)}, f32[2,2,8,8,128]{4,3,2,1,0:T(8,128)S(1)}, u32[]{:S(2)}, u32[]{:S(2)}) %collective-permute-start.1) | collective-permute-done | bytes 131104 | tf_op jit(solution)/shard_map/ppermute | solution.py:212
  16.0 2.5 %collective-permute-done.3 = f32[2,2,8,8,128]{4,3,2,1,0:T(8,128)S(1)} collective-permute-done((f32[2,2,8,8,128]{4,3,2,1,0:T(8,128)S(1)}, f32[2,2,8,8,128]{4,3,2,1,0:T(8,128)S(1)}, u32[]{:S(2)}, u32[]{:S(2)}) %collective-permute-start.3) | collective-permute-done | bytes 131104 | tf_op jit(solution)/shard_map/ppermute | solution.py:212
  18.5 0.3 collective-permute-done.2
  18.8 7.3 %collective-permute-start.4 = (f32[2,8,8,128]{3,2,1,0:T(8,128)S(1)}, f32[2,8,8,128]{3,2,1,0:T(8,128)S(1)}, u32[]{:S(2)}, u32[]{:S(2)}) collective-permute-start(f32[2,8,8,128]{3,2,1,0:T(8,128)S(1)} %get-tuple-element.12), channel_id=1, source_target_pairs={{0,2},{2,0},{1,3},{3,1},{4,6},{6,4},{5,7},{7,5},{8,10},{10,8},{9,1... | collective-permute-start | bytes 196616 | tf_op jit(solution)/shard_map/ppermute | solution.py:212
  26.1 2.3 %collective-permute-done.4.came_ref = f32[2,8,8,128]{3,2,1,0:T(8,128)S(1)} collective-permute-done((f32[2,8,8,128]{3,2,1,0:T(8,128)S(1)}, f32[2,8,8,128]{3,2,1,0:T(8,128)S(1)}, u32[]{:S(2)}, u32[]{:S(2)}) %collective-permute-start.4) | collective-permute-done | bytes 65568 | tf_op jit(solution)/shard_map/ppermute | solution.py:212
  28.4 0.1 turn.1.own_ref
  28.6 3.3 %collective-permute-start.9 = (f32[4,32,128]{2,1,0:T(8,128)S(1)}, f32[4,32,128]{2,1,0:T(8,128)S(1)}, u32[]{:S(2)}, u32[]{:S(2)}) collective-permute-start(f32[4,32,128]{2,1,0:T(8,128)S(1)} %turn.1.own_ref), channel_id=1, source_target_pairs={{0,48},{16,32},{32,16},{48,0},{1,49},{17,33},{33,17},{49,1},{2,50}... | collective-permute-start | bytes 196616 | tf_op jit(solution)/shard_map/ppermute | solution.py:216
  31.9 0.0 collective-permute-start.8
  31.9 0.5 collective-permute-start.7
  32.4 2.4 %collective-permute-start.6 = (f32[4,32,128]{2,1,0:T(8,128)S(1)}, f32[4,32,128]{2,1,0:T(8,128)S(1)}, u32[]{:S(2)}, u32[]{:S(2)}) collective-permute-start(f32[4,32,128]{2,1,0:T(8,128)S(1)} %turn.1.own_ref), channel_id=1, source_target_pairs={{0,128},{64,192},{128,0},{192,64},{1,129},{65,193},{129,1},{193,65... | collective-permute-start | bytes 196616 | tf_op jit(solution)/shard_map/ppermute | solution.py:216
  34.8 1.2 %collective-permute-start.5 = (f32[4,32,128]{2,1,0:T(8,128)S(1)}, f32[4,32,128]{2,1,0:T(8,128)S(1)}, u32[]{:S(2)}, u32[]{:S(2)}) collective-permute-start(f32[4,32,128]{2,1,0:T(8,128)S(1)} %turn.1.own_ref), channel_id=1, source_target_pairs={{0,64},{64,0},{128,192},{192,128},{1,65},{65,1},{129,193},{193,129... | collective-permute-start | bytes 196616 | tf_op jit(solution)/shard_map/ppermute | solution.py:216
  36.0 0.0 collective-permute-done.9
  36.0 1.2 %collective-permute-done.8 = f32[4,32,128]{2,1,0:T(8,128)S(1)} collective-permute-done((f32[4,32,128]{2,1,0:T(8,128)S(1)}, f32[4,32,128]{2,1,0:T(8,128)S(1)}, u32[]{:S(2)}, u32[]{:S(2)}) %collective-permute-start.8) | collective-permute-done | bytes 65568 | tf_op jit(solution)/shard_map/ppermute | solution.py:216
  37.3 0.6 %collective-permute-start.13 = (f32[2,4,32,128]{3,2,1,0:T(8,128)S(1)}, f32[2,4,32,128]{3,2,1,0:T(8,128)S(1)}, u32[]{:S(2)}, u32[]{:S(2)}) collective-permute-start(f32[2,4,32,128]{3,2,1,0:T(8,128)S(1)} %pad_maximum_fusion.1), channel_id=1, source_target_pairs={{0,192},{64,128},{128,64},{192,0},{1,193},{65,129},{129,65},{193,1... | collective-permute-start | bytes 393224 | tf_op jit(solution)/shard_map/ppermute | solution.py:216
  37.8 0.9 %collective-permute-start.12 = (f32[2,4,32,128]{3,2,1,0:T(8,128)S(1)}, f32[2,4,32,128]{3,2,1,0:T(8,128)S(1)}, u32[]{:S(2)}, u32[]{:S(2)}) collective-permute-start(f32[2,4,32,128]{3,2,1,0:T(8,128)S(1)} %pad_maximum_fusion.1), channel_id=1, source_target_pairs={{0,64},{64,0},{128,192},{192,128},{1,65},{65,1},{129,193},{193,129... | collective-permute-start | bytes 393224 | tf_op jit(solution)/shard_map/ppermute | solution.py:216
  38.7 0.0 collective-permute-done.7
  38.7 3.3 %collective-permute-start.11 = (f32[2,4,32,128]{3,2,1,0:T(8,128)S(1)}, f32[2,4,32,128]{3,2,1,0:T(8,128)S(1)}, u32[]{:S(2)}, u32[]{:S(2)}) collective-permute-start(f32[2,4,32,128]{3,2,1,0:T(8,128)S(1)} %pad_maximum_fusion.1), channel_id=1, source_target_pairs={{0,128},{64,192},{128,0},{192,64},{1,129},{65,193},{129,1},{193,65... | collective-permute-start | bytes 393224 | tf_op jit(solution)/shard_map/ppermute | solution.py:216
  42.0 0.0 collective-permute-done.6
  42.1 0.0 collective-permute-done.5
  42.1 0.1 collective-permute-start.10
  42.3 1.9 %collective-permute-done.13.refs_4_ = f32[2,4,32,128]{3,2,1,0:T(8,128)S(1)} collective-permute-done((f32[2,4,32,128]{3,2,1,0:T(8,128)S(1)}, f32[2,4,32,128]{3,2,1,0:T(8,128)S(1)}, u32[]{:S(2)}, u32[]{:S(2)}) %collective-permute-start.13) | collective-permute-done | bytes 131104 | tf_op jit(solution)/shard_map/ppermute | solution.py:216
  44.2 0.0 collective-permute-done.12.refs_3_
  44.2 2.2 %collective-permute-done.11.refs_2_ = f32[2,4,32,128]{3,2,1,0:T(8,128)S(1)} collective-permute-done((f32[2,4,32,128]{3,2,1,0:T(8,128)S(1)}, f32[2,4,32,128]{3,2,1,0:T(8,128)S(1)}, u32[]{:S(2)}, u32[]{:S(2)}) %collective-permute-start.11) | collective-permute-done | bytes 131104 | tf_op jit(solution)/shard_map/ppermute | solution.py:216
  46.4 2.1 %collective-permute-done.10.refs_1_ = f32[4,4,32,128]{3,2,1,0:T(8,128)S(1)} collective-permute-done((f32[4,4,32,128]{3,2,1,0:T(8,128)S(1)}, f32[4,4,32,128]{3,2,1,0:T(8,128)S(1)}, u32[]{:S(2)}, u32[]{:S(2)}) %collective-permute-start.10) | collective-permute-done | bytes 262176 | tf_op jit(solution)/shard_map/ppermute | solution.py:216
  48.5 1.8 %gram.1 = f32[2,8,32,512]{3,2,1,0:T(8,128)} custom-call(s32[6]{0:T(128)S(1)} %stack.61.place, f32[4,32,128]{2,1,0:T(8,128)S(1)} %turn.1.own_ref, f32[6,4,32,128]{3,2,1,0:T(8,128)S(1)} %constant_dynamic-update-slice_fusion.refs_0_, f32[4,4,32,128]{3,2,1,0:T(8,128)S(1)} %collective-permute-done.10.refs_1_, ...), custom_call_target="tpu_custom_call" | custom-call | tf_op jit(solution)/shard_map/gram/pallas_call | solution.py:195
  (11 shorter events, 0.1 us)
Async XLA Ops:
  6.1 2.0 %collective-permute-start = (f32[4,2,2,8,8,128]{5,4,3,2,1,0:T(8,128)S(1)}, f32[4,2,2,8,8,128]{5,4,3,2,1,0:T(8,128)S(1)}, u32[]{:S(2)}, u32[]{:S(2)}) collective-permute-start(f32[4,2,2,8,8,128]{5,4,3,2,1,0:T(8,128)S(1)} %get-tuple-element.8), channel_id=1, source_target_pairs={{0,1},{1,0},{2,3},{3,2},{4,5},{5,4},{6,7},{7,6},{8,9},{9,8},{10,11... | collective-permute-start | bytes 1572872 | tf_op jit(solution)/shard_map/ppermute | solution.py:212
  8.2 7.8 %collective-permute-start.1 = (f32[2,2,8,8,128]{4,3,2,1,0:T(8,128)S(1)}, f32[2,2,8,8,128]{4,3,2,1,0:T(8,128)S(1)}, u32[]{:S(2)}, u32[]{:S(2)}) collective-permute-start(f32[2,2,8,8,128]{4,3,2,1,0:T(8,128)S(1)} %get-tuple-element.9), channel_id=1, source_target_pairs={{0,8},{4,12},{8,0},{12,4},{1,9},{5,13},{9,1},{13,5},{2,10},{6,14},... | collective-permute-start | bytes 393224 | tf_op jit(solution)/shard_map/ppermute | solution.py:212
  11.5 7.0 %collective-permute-start.3 = (f32[2,2,8,8,128]{4,3,2,1,0:T(8,128)S(1)}, f32[2,2,8,8,128]{4,3,2,1,0:T(8,128)S(1)}, u32[]{:S(2)}, u32[]{:S(2)}) collective-permute-start(f32[2,2,8,8,128]{4,3,2,1,0:T(8,128)S(1)} %get-tuple-element.10), channel_id=1, source_target_pairs={{0,12},{4,0},{8,4},{12,8},{1,13},{5,1},{9,5},{13,9},{2,14},{6,2},{... | collective-permute-start | bytes 393224 | tf_op jit(solution)/shard_map/ppermute | solution.py:212
  12.5 6.2 %collective-permute-start.2 = (f32[2,2,8,8,128]{4,3,2,1,0:T(8,128)S(1)}, f32[2,2,8,8,128]{4,3,2,1,0:T(8,128)S(1)}, u32[]{:S(2)}, u32[]{:S(2)}) collective-permute-start(f32[2,2,8,8,128]{4,3,2,1,0:T(8,128)S(1)} %get-tuple-element.11), channel_id=1, source_target_pairs={{0,4},{4,8},{8,12},{12,0},{1,5},{5,9},{9,13},{13,1},{2,6},{6,10},{... | collective-permute-start | bytes 393224 | tf_op jit(solution)/shard_map/ppermute | solution.py:212
  18.8 9.6 %collective-permute-start.4 = (f32[2,8,8,128]{3,2,1,0:T(8,128)S(1)}, f32[2,8,8,128]{3,2,1,0:T(8,128)S(1)}, u32[]{:S(2)}, u32[]{:S(2)}) collective-permute-start(f32[2,8,8,128]{3,2,1,0:T(8,128)S(1)} %get-tuple-element.12), channel_id=1, source_target_pairs={{0,2},{2,0},{1,3},{3,1},{4,6},{6,4},{5,7},{7,5},{8,10},{10,8},{9,1... | collective-permute-start | bytes 196616 | tf_op jit(solution)/shard_map/ppermute | solution.py:212
  28.6 7.5 %collective-permute-start.9 = (f32[4,32,128]{2,1,0:T(8,128)S(1)}, f32[4,32,128]{2,1,0:T(8,128)S(1)}, u32[]{:S(2)}, u32[]{:S(2)}) collective-permute-start(f32[4,32,128]{2,1,0:T(8,128)S(1)} %turn.1.own_ref), channel_id=1, source_target_pairs={{0,48},{16,32},{32,16},{48,0},{1,49},{17,33},{33,17},{49,1},{2,50}... | collective-permute-start | bytes 196616 | tf_op jit(solution)/shard_map/ppermute | solution.py:216
  31.9 5.3 %collective-permute-start.8 = (f32[4,32,128]{2,1,0:T(8,128)S(1)}, f32[4,32,128]{2,1,0:T(8,128)S(1)}, u32[]{:S(2)}, u32[]{:S(2)}) collective-permute-start(f32[4,32,128]{2,1,0:T(8,128)S(1)} %turn.1.own_ref), channel_id=1, source_target_pairs={{0,32},{16,48},{32,0},{48,16},{1,33},{17,49},{33,1},{49,17},{2,34}... | collective-permute-start | bytes 196616 | tf_op jit(solution)/shard_map/ppermute | solution.py:216
  31.9 6.8 %collective-permute-start.7 = (f32[4,32,128]{2,1,0:T(8,128)S(1)}, f32[4,32,128]{2,1,0:T(8,128)S(1)}, u32[]{:S(2)}, u32[]{:S(2)}) collective-permute-start(f32[4,32,128]{2,1,0:T(8,128)S(1)} %turn.1.own_ref), channel_id=1, source_target_pairs={{0,192},{64,128},{128,64},{192,0},{1,193},{65,129},{129,65},{193,1... | collective-permute-start | bytes 196616 | tf_op jit(solution)/shard_map/ppermute | solution.py:216
  32.4 9.6 %collective-permute-start.6 = (f32[4,32,128]{2,1,0:T(8,128)S(1)}, f32[4,32,128]{2,1,0:T(8,128)S(1)}, u32[]{:S(2)}, u32[]{:S(2)}) collective-permute-start(f32[4,32,128]{2,1,0:T(8,128)S(1)} %turn.1.own_ref), channel_id=1, source_target_pairs={{0,128},{64,192},{128,0},{192,64},{1,129},{65,193},{129,1},{193,65... | collective-permute-start | bytes 196616 | tf_op jit(solution)/shard_map/ppermute | solution.py:216
  34.8 7.2 %collective-permute-start.5 = (f32[4,32,128]{2,1,0:T(8,128)S(1)}, f32[4,32,128]{2,1,0:T(8,128)S(1)}, u32[]{:S(2)}, u32[]{:S(2)}) collective-permute-start(f32[4,32,128]{2,1,0:T(8,128)S(1)} %turn.1.own_ref), channel_id=1, source_target_pairs={{0,64},{64,0},{128,192},{192,128},{1,65},{65,1},{129,193},{193,129... | collective-permute-start | bytes 196616 | tf_op jit(solution)/shard_map/ppermute | solution.py:216
  37.3 6.9 %collective-permute-start.13 = (f32[2,4,32,128]{3,2,1,0:T(8,128)S(1)}, f32[2,4,32,128]{3,2,1,0:T(8,128)S(1)}, u32[]{:S(2)}, u32[]{:S(2)}) collective-permute-start(f32[2,4,32,128]{3,2,1,0:T(8,128)S(1)} %pad_maximum_fusion.1), channel_id=1, source_target_pairs={{0,192},{64,128},{128,64},{192,0},{1,193},{65,129},{129,65},{193,1... | collective-permute-start | bytes 393224 | tf_op jit(solution)/shard_map/ppermute | solution.py:216
  37.8 6.4 %collective-permute-start.12 = (f32[2,4,32,128]{3,2,1,0:T(8,128)S(1)}, f32[2,4,32,128]{3,2,1,0:T(8,128)S(1)}, u32[]{:S(2)}, u32[]{:S(2)}) collective-permute-start(f32[2,4,32,128]{3,2,1,0:T(8,128)S(1)} %pad_maximum_fusion.1), channel_id=1, source_target_pairs={{0,64},{64,0},{128,192},{192,128},{1,65},{65,1},{129,193},{193,129... | collective-permute-start | bytes 393224 | tf_op jit(solution)/shard_map/ppermute | solution.py:216
  38.7 7.7 %collective-permute-start.11 = (f32[2,4,32,128]{3,2,1,0:T(8,128)S(1)}, f32[2,4,32,128]{3,2,1,0:T(8,128)S(1)}, u32[]{:S(2)}, u32[]{:S(2)}) collective-permute-start(f32[2,4,32,128]{3,2,1,0:T(8,128)S(1)} %pad_maximum_fusion.1), channel_id=1, source_target_pairs={{0,128},{64,192},{128,0},{192,64},{1,129},{65,193},{129,1},{193,65... | collective-permute-start | bytes 393224 | tf_op jit(solution)/shard_map/ppermute | solution.py:216
  42.1 6.5 %collective-permute-start.10 = (f32[4,4,32,128]{3,2,1,0:T(8,128)S(1)}, f32[4,4,32,128]{3,2,1,0:T(8,128)S(1)}, u32[]{:S(2)}, u32[]{:S(2)}) collective-permute-start(f32[4,4,32,128]{3,2,1,0:T(8,128)S(1)} %pad_maximum_fusion), channel_id=1, source_target_pairs={{0,16},{16,0},{32,48},{48,32},{1,17},{17,1},{33,49},{49,33},{2,18}... | collective-permute-start | bytes 786440 | tf_op jit(solution)/shard_map/ppermute | solution.py:216

commit v3 on v2

--- a/solution.py
+++ b/solution.py
@@ -48,7 +48,7 @@
 CHUNKS = (2, 2, 2, 2)
 
 
-def dft_kernel(place, kx_hbm, kz_hbm, signal, mine, other, held, basis, kx_ref, kz_ref, sems):
+def dft_kernel(place, kx_hbm, kz_hbm, signal, own_mine, own_other, far_mine, far_other, held, basis, kx_ref, kz_ref, sems):
     modes, parts, quads, groups, snaps, width = signal.shape
     pairs = kx_ref.shape[1]
     index = [
@@ -89,12 +89,15 @@
             turned = total[i * 128 : (i + 1) * 128].T
             for yy in range(4):
                 slot = (yy + 4 - y) & 3
-                for zz in range(2):
-                    for c in range(parts):
+                for c in range(parts):
+                    tiles = []
+                    for zz in range(2):
                         at = c * pairs + (yy * 4 + zz * 2) * 8
                         low, high = turned[at : at + 8], turned[at + 8 : at + 16]
-                        mine[slot, zz ^ zh, c, first + i] = jnp.where(core == 0, low, high)
-                        other[slot, zz ^ zh, c, first + i] = jnp.where(core == 0, high, low)
+                        tiles.append((jnp.where(core == 0, low, high), jnp.where(core == 0, high, low)))
+                    for n, (own, far) in enumerate(((own_mine, far_mine), (own_other, far_other))):
+                        own[slot, c, first + i] = jnp.where(zh == 0, tiles[0][n], tiles[1][n])
+                        far[slot, c, first + i] = jnp.where(zh == 0, tiles[1][n], tiles[0][n])
         first += size
 
 
@@ -102,12 +105,12 @@
     modes, parts, planes, snaps, width = signal.shape
     pairs = kx_index.shape[0]
     view = signal.reshape(modes, parts, 4, planes // 4, snaps, width)
-    block = jax.ShapeDtypeStruct((4, 2, parts, planes // 4, 8, 128), jnp.float32)
+    block = jax.ShapeDtypeStruct((4, parts, planes // 4, 8, 128), jnp.float32)
     return pl.pallas_call(
         dft_kernel,
-        out_shape=(block, block),
+        out_shape=(block,) * 4,
         in_specs=[SMEM, FAR, FAR, HBM],
-        out_specs=(VMEM, VMEM),
+        out_specs=(VMEM,) * 4,
         scratch_shapes=[
             pltpu.VMEM(view.shape, signal.dtype),
             pltpu.VMEM((parts * width, 2 * pairs), jnp.bfloat16),
@@ -218,15 +221,21 @@
 
 def gathered(own):
     z3, z2 = (swapped(own, "zl", j) for j in (3, 2))
-    x2, x1, x3 = (swapped(own, "x", i) for i in (2, 1, 3))
+    x1, x2, x3 = (swapped(own, "x", i) for i in (1, 2, 3))
     blocks = [jnp.stack([own, x1, x2, x3, z2, z3])]
     spots = [[(0, 0), (1, 0), (2, 0), (3, 0), (0, 2), (0, 3)]]
     blocks.append(swapped(blocks[0][:4], "zl", 1))
     spots.append([(i, 1) for i in range(4)])
-    for i in (2, 1, 3):
+    for i in (1, 2, 3):
         blocks.append(swapped(jnp.stack([z2, z3]), "x", i))
         spots.append([(i, 2), (i, 3)])
     return blocks, spots
+
+
+def summed_over_y(mine, other):
+    summed = mine + swapped(other, "core", 1)
+    came = [shifted(summed[i], "y", i) for i in (1, 2, 3)]
+    return summed[0] + came[0] + came[1] + came[2]
 
 
 def on_device(signal, kx_index, kz_index):
@@ -234,11 +243,10 @@
     y, zh, core = (lax.axis_index(name) for name in SPEC)
     at = lax.axis_index(SPEC) * width
     place = jnp.stack([at, y, zh, core, lax.axis_index("x"), lax.axis_index("zl")]).astype(jnp.int32)
-    mine, other = dft(place, kx_index, kz_index, signal)
-    summed = mine + shifted(other, "core", 1)
-    came = [shifted(summed[i], "y", i) for i in (2, 1, 3)]
-    halves = summed[0] + came[0] + came[1] + came[2]
-    own = turn(halves[0], shifted(halves[1], "zh", 1))
+    own_mine, own_other, far_mine, far_other = dft(place, kx_index, kz_index, signal)
+    far = summed_over_y(far_mine, far_other)
+    came = swapped(far, "zh", 1)
+    own = turn(summed_over_y(own_mine, own_other), came)
     return gram(place, own, *gathered(own))
 
 

time: 50.4 us -> 48.7 us (0.966)
  waiting for transfers between devices: 17 us -> 11.1 us
  starting transfers between devices: 25 us -> 29.2 us
    ppermute x5 -> x6, waiting for transfers between devices: 9.49 us -> 0.34 us  [shifted(): lax.ppermute(array, axis, [(s, (s + by) % size) for s in range(size)])]
    ppermute x9 -> x12, starting transfers between devices: 12.3 us -> 20.2 us  [swapped(): lax.ppermute(array, axis, [(s, s ^ by) for s in range(lax.axis_size(axis))])]
    ppermute x5 -> x6, starting transfers between devices: 12.7 us -> 8.95 us  [shifted(): lax.ppermute(array, axis, [(s, (s + by) % size) for s in range(size)])]
    ppermute x9 -> x12, waiting for transfers between devices: 7.5 us -> 10.7 us  [swapped(): lax.ppermute(array, axis, [(s, s ^ by) for s in range(lax.axis_size(axis))])]
  transfers between devices with their start and end apart: 14 -> 18, of which waited for: 9 -> 7; matrix products, arithmetic and copies ran while one was open for 0% -> 0% of each run, Pallas kernels for 0% -> 0%
where the time goes in v3:
time: 48.7 us; the launch traced here: 48.6 us
  starting transfers between devices  29.2 us (60%)
  waiting for transfers between devices  11.1 us (23%)
  Pallas kernels  7.96 us (16%)
    ppermute x12, starting transfers between devices, swapped(): lax.ppermute(array, axis, [(s, s ^ by) for s in range(lax.axis_size(axis))])  20.2 us
    ppermute x12, waiting for transfers between devices, swapped(): lax.ppermute(array, axis, [(s, s ^ by) for s in range(lax.axis_size(axis))])  10.7 us
    ppermute x6, starting transfers between devices, shifted(): lax.ppermute(array, axis, [(s, (s + by) % size) for s in range(size)])  8.95 us
    pallas_call x1, Pallas kernels, dft(): pl.pallas_call(dft_kernel, out_shape=(block,) * 4, in_specs=[SMEM, FAR, F...  6.02 us
    pallas_call x1, Pallas kernels, gram(): pl.pallas_call(functools.partial(gram_kernel, spots), out_shape=jax.Shape...  1.82 us
  transfers between devices with their start and end apart: 18, of which 7 were waited for; matrix products, arithmetic and copies ran while one was open for 0% of the time, Pallas kernels for 0%

profile of v3, /device:TPU:6, one launch (start us, length us, event | category | flops | bytes accessed | tf_op | source)
XLA Modules:
  0.0 48.6 jit_solution(3055001705610703384)
XLA Ops:
  0.0 0.1 stack.61.place
  0.1 6.0 %dft.1 = (f32[4,2,8,8,128]{4,3,2,1,0:T(8,128)S(1)}, f32[4,2,8,8,128]{4,3,2,1,0:T(8,128)S(1)}, f32[4,2,8,8,128]{4,3,2,1,0:T(8,128)S(1)}, f32[4,2,8,8,128]{4,3,2,1,0:T(8,128)S(1)}) custom-call(s32[6]{0:T(128)S(1)} %stack.61.place, s32[1,128]{1,0:T(1,128)} %bitcast.56, s32[1,128]{1,0:T(1,128)} %bitcast.57, bf16[4,2,4,8,32,640]{5,4,3,2,1,0:T(8,128)(2,1)} %bitcast.50), custom_call_target="tpu_custom_call" | custom-call | tf_op jit(solution)/shard_map/dft/pallas_call | solution.py:109
  6.1 0.1 collective-permute-start.4
  6.2 0.5 %collective-permute-start = (f32[4,2,8,8,128]{4,3,2,1,0:T(8,128)S(1)}, f32[4,2,8,8,128]{4,3,2,1,0:T(8,128)S(1)}, u32[]{:S(2)}, u32[]{:S(2)}) collective-permute-start(f32[4,2,8,8,128]{4,3,2,1,0:T(8,128)S(1)} %get-tuple-element.10), channel_id=1, source_target_pairs={{0,1},{1,0},{2,3},{3,2},{4,5},{5,4},{6,7},{7,6},{8,9},{9,8},{10,11... | collective-permute-start | bytes 786440 | tf_op jit(solution)/shard_map/ppermute | solution.py:219
  6.7 1.0 %collective-permute-done.4 = f32[4,2,8,8,128]{4,3,2,1,0:T(8,128)S(1)} collective-permute-done((f32[4,2,8,8,128]{4,3,2,1,0:T(8,128)S(1)}, f32[4,2,8,8,128]{4,3,2,1,0:T(8,128)S(1)}, u32[]{:S(2)}, u32[]{:S(2)}) %collective-permute-start.4) | collective-permute-done | bytes 262176 | tf_op jit(solution)/shard_map/ppermute | solution.py:219
  7.8 1.7 %collective-permute-start.5 = (f32[2,8,8,128]{3,2,1,0:T(8,128)S(1)}, f32[2,8,8,128]{3,2,1,0:T(8,128)S(1)}, u32[]{:S(2)}, u32[]{:S(2)}) collective-permute-start(f32[2,8,8,128]{3,2,1,0:T(8,128)S(1)} %get-tuple-element.13), channel_id=1, source_target_pairs={{0,4},{4,8},{8,12},{12,0},{1,5},{5,9},{9,13},{13,1},{2,6},{6,10},{... | collective-permute-start | bytes 196616 | tf_op jit(solution)/shard_map/ppermute | solution.py:215
  9.5 1.7 %collective-permute-start.7 = (f32[2,8,8,128]{3,2,1,0:T(8,128)S(1)}, f32[2,8,8,128]{3,2,1,0:T(8,128)S(1)}, u32[]{:S(2)}, u32[]{:S(2)}) collective-permute-start(f32[2,8,8,128]{3,2,1,0:T(8,128)S(1)} %get-tuple-element.14), channel_id=1, source_target_pairs={{0,12},{4,0},{8,4},{12,8},{1,13},{5,1},{9,5},{13,9},{2,14},{6,2},{... | collective-permute-start | bytes 196616 | tf_op jit(solution)/shard_map/ppermute | solution.py:215
  11.1 2.0 %collective-permute-start.6 = (f32[2,8,8,128]{3,2,1,0:T(8,128)S(1)}, f32[2,8,8,128]{3,2,1,0:T(8,128)S(1)}, u32[]{:S(2)}, u32[]{:S(2)}) collective-permute-start(f32[2,8,8,128]{3,2,1,0:T(8,128)S(1)} %get-tuple-element.15), channel_id=1, source_target_pairs={{0,8},{4,12},{8,0},{12,4},{1,9},{5,13},{9,1},{13,5},{2,10},{6,14},... | collective-permute-start | bytes 196616 | tf_op jit(solution)/shard_map/ppermute | solution.py:215
  13.1 0.0 collective-permute-done
  13.2 0.8 %collective-permute-start.1 = (f32[2,8,8,128]{3,2,1,0:T(8,128)S(1)}, f32[2,8,8,128]{3,2,1,0:T(8,128)S(1)}, u32[]{:S(2)}, u32[]{:S(2)}) collective-permute-start(f32[2,8,8,128]{3,2,1,0:T(8,128)S(1)} %get-tuple-element.16), channel_id=1, source_target_pairs={{0,4},{4,8},{8,12},{12,0},{1,5},{5,9},{9,13},{13,1},{2,6},{6,10},{... | collective-permute-start | bytes 196616 | tf_op jit(solution)/shard_map/ppermute | solution.py:215
  13.9 2.6 %collective-permute-start.3 = (f32[2,8,8,128]{3,2,1,0:T(8,128)S(1)}, f32[2,8,8,128]{3,2,1,0:T(8,128)S(1)}, u32[]{:S(2)}, u32[]{:S(2)}) collective-permute-start(f32[2,8,8,128]{3,2,1,0:T(8,128)S(1)} %get-tuple-element.17), channel_id=1, source_target_pairs={{0,12},{4,0},{8,4},{12,8},{1,13},{5,1},{9,5},{13,9},{2,14},{6,2},{... | collective-permute-start | bytes 196616 | tf_op jit(solution)/shard_map/ppermute | solution.py:215
  16.5 0.0 collective-permute-done.5
  16.5 0.3 collective-permute-start.2
  16.8 0.0 collective-permute-done.7
  16.8 0.3 collective-permute-done.6
  17.2 7.3 %collective-permute-start.8 = (f32[2,8,8,128]{3,2,1,0:T(8,128)S(1)}, f32[2,8,8,128]{3,2,1,0:T(8,128)S(1)}, u32[]{:S(2)}, u32[]{:S(2)}) collective-permute-start(f32[2,8,8,128]{3,2,1,0:T(8,128)S(1)} %fusion.2), channel_id=1, source_target_pairs={{0,2},{2,0},{1,3},{3,1},{4,6},{6,4},{5,7},{7,5},{8,10},{10,8},{9,1... | collective-permute-start | bytes 196616 | tf_op jit(solution)/shard_map/ppermute | solution.py:219
  24.4 0.0 collective-permute-done.1
  24.4 0.0 collective-permute-done.3
  24.4 0.0 collective-permute-done.2
  24.5 2.3 %collective-permute-done.8.came_ref = f32[2,8,8,128]{3,2,1,0:T(8,128)S(1)} collective-permute-done((f32[2,8,8,128]{3,2,1,0:T(8,128)S(1)}, f32[2,8,8,128]{3,2,1,0:T(8,128)S(1)}, u32[]{:S(2)}, u32[]{:S(2)}) %collective-permute-start.8) | collective-permute-done | bytes 65568 | tf_op jit(solution)/shard_map/ppermute | solution.py:219
  26.8 0.1 turn.1.own_ref
  26.9 4.0 %collective-permute-start.13 = (f32[4,32,128]{2,1,0:T(8,128)S(1)}, f32[4,32,128]{2,1,0:T(8,128)S(1)}, u32[]{:S(2)}, u32[]{:S(2)}) collective-permute-start(f32[4,32,128]{2,1,0:T(8,128)S(1)} %turn.1.own_ref), channel_id=1, source_target_pairs={{0,48},{16,32},{32,16},{48,0},{1,49},{17,33},{33,17},{49,1},{2,50}... | collective-permute-start | bytes 196616 | tf_op jit(solution)/shard_map/ppermute | solution.py:219
  31.0 0.0 collective-permute-start.12
  31.0 0.5 collective-permute-start.11
  31.4 2.4 %collective-permute-start.10 = (f32[4,32,128]{2,1,0:T(8,128)S(1)}, f32[4,32,128]{2,1,0:T(8,128)S(1)}, u32[]{:S(2)}, u32[]{:S(2)}) collective-permute-start(f32[4,32,128]{2,1,0:T(8,128)S(1)} %turn.1.own_ref), channel_id=1, source_target_pairs={{0,128},{64,192},{128,0},{192,64},{1,129},{65,193},{129,1},{193,65... | collective-permute-start | bytes 196616 | tf_op jit(solution)/shard_map/ppermute | solution.py:219
  33.9 1.2 %collective-permute-start.9 = (f32[4,32,128]{2,1,0:T(8,128)S(1)}, f32[4,32,128]{2,1,0:T(8,128)S(1)}, u32[]{:S(2)}, u32[]{:S(2)}) collective-permute-start(f32[4,32,128]{2,1,0:T(8,128)S(1)} %turn.1.own_ref), channel_id=1, source_target_pairs={{0,64},{64,0},{128,192},{192,128},{1,65},{65,1},{129,193},{193,129... | collective-permute-start | bytes 196616 | tf_op jit(solution)/shard_map/ppermute | solution.py:219
  35.1 0.0 collective-permute-done.13
  35.1 1.1 %collective-permute-done.12 = f32[4,32,128]{2,1,0:T(8,128)S(1)} collective-permute-done((f32[4,32,128]{2,1,0:T(8,128)S(1)}, f32[4,32,128]{2,1,0:T(8,128)S(1)}, u32[]{:S(2)}, u32[]{:S(2)}) %collective-permute-start.12) | collective-permute-done | bytes 65568 | tf_op jit(solution)/shard_map/ppermute | solution.py:219
  36.1 0.6 %collective-permute-start.17 = (f32[2,4,32,128]{3,2,1,0:T(8,128)S(1)}, f32[2,4,32,128]{3,2,1,0:T(8,128)S(1)}, u32[]{:S(2)}, u32[]{:S(2)}) collective-permute-start(f32[2,4,32,128]{3,2,1,0:T(8,128)S(1)} %pad_maximum_fusion.1), channel_id=1, source_target_pairs={{0,192},{64,128},{128,64},{192,0},{1,193},{65,129},{129,65},{193,1... | collective-permute-start | bytes 393224 | tf_op jit(solution)/shard_map/ppermute | solution.py:219
  36.7 2.4 %collective-permute-start.16 = (f32[2,4,32,128]{3,2,1,0:T(8,128)S(1)}, f32[2,4,32,128]{3,2,1,0:T(8,128)S(1)}, u32[]{:S(2)}, u32[]{:S(2)}) collective-permute-start(f32[2,4,32,128]{3,2,1,0:T(8,128)S(1)} %pad_maximum_fusion.1), channel_id=1, source_target_pairs={{0,128},{64,192},{128,0},{192,64},{1,129},{65,193},{129,1},{193,65... | collective-permute-start | bytes 393224 | tf_op jit(solution)/shard_map/ppermute | solution.py:219
  39.1 0.0 collective-permute-done.11
  39.2 1.2 %collective-permute-start.15 = (f32[2,4,32,128]{3,2,1,0:T(8,128)S(1)}, f32[2,4,32,128]{3,2,1,0:T(8,128)S(1)}, u32[]{:S(2)}, u32[]{:S(2)}) collective-permute-start(f32[2,4,32,128]{3,2,1,0:T(8,128)S(1)} %pad_maximum_fusion.1), channel_id=1, source_target_pairs={{0,64},{64,0},{128,192},{192,128},{1,65},{65,1},{129,193},{193,129... | collective-permute-start | bytes 393224 | tf_op jit(solution)/shard_map/ppermute | solution.py:219
  40.3 0.0 collective-permute-done.10
  40.3 0.0 collective-permute-done.9
  40.4 0.1 collective-permute-start.14
  40.5 3.3 %collective-permute-done.17.refs_4_ = f32[2,4,32,128]{3,2,1,0:T(8,128)S(1)} collective-permute-done((f32[2,4,32,128]{3,2,1,0:T(8,128)S(1)}, f32[2,4,32,128]{3,2,1,0:T(8,128)S(1)}, u32[]{:S(2)}, u32[]{:S(2)}) %collective-permute-start.17) | collective-permute-done | bytes 131104 | tf_op jit(solution)/shard_map/ppermute | solution.py:219
  43.8 0.0 collective-permute-done.16.refs_3_
  43.8 0.9 %collective-permute-done.15.refs_2_ = f32[2,4,32,128]{3,2,1,0:T(8,128)S(1)} collective-permute-done((f32[2,4,32,128]{3,2,1,0:T(8,128)S(1)}, f32[2,4,32,128]{3,2,1,0:T(8,128)S(1)}, u32[]{:S(2)}, u32[]{:S(2)}) %collective-permute-start.15) | collective-permute-done | bytes 131104 | tf_op jit(solution)/shard_map/ppermute | solution.py:219
  44.7 2.1 %collective-permute-done.14.refs_1_ = f32[4,4,32,128]{3,2,1,0:T(8,128)S(1)} collective-permute-done((f32[4,4,32,128]{3,2,1,0:T(8,128)S(1)}, f32[4,4,32,128]{3,2,1,0:T(8,128)S(1)}, u32[]{:S(2)}, u32[]{:S(2)}) %collective-permute-start.14) | collective-permute-done | bytes 262176 | tf_op jit(solution)/shard_map/ppermute | solution.py:219
  46.8 1.8 %gram.1 = f32[2,8,32,512]{3,2,1,0:T(8,128)} custom-call(s32[6]{0:T(128)S(1)} %stack.61.place, f32[4,32,128]{2,1,0:T(8,128)S(1)} %turn.1.own_ref, f32[6,4,32,128]{3,2,1,0:T(8,128)S(1)} %constant_dynamic-update-slice_fusion.refs_0_, f32[4,4,32,128]{3,2,1,0:T(8,128)S(1)} %collective-permute-done.14.refs_1_, ...), custom_call_target="tpu_custom_call" | custom-call | tf_op jit(solution)/shard_map/gram/pallas_call | solution.py:198
  (14 shorter events, 0.2 us)
Async XLA Ops:
  6.1 1.6 %collective-permute-start.4 = (f32[4,2,8,8,128]{4,3,2,1,0:T(8,128)S(1)}, f32[4,2,8,8,128]{4,3,2,1,0:T(8,128)S(1)}, u32[]{:S(2)}, u32[]{:S(2)}) collective-permute-start(f32[4,2,8,8,128]{4,3,2,1,0:T(8,128)S(1)} %get-tuple-element.12), channel_id=1, source_target_pairs={{0,1},{1,0},{2,3},{3,2},{4,5},{5,4},{6,7},{7,6},{8,9},{9,8},{10,11... | collective-permute-start | bytes 786440 | tf_op jit(solution)/shard_map/ppermute | solution.py:219
  6.2 6.9 %collective-permute-start = (f32[4,2,8,8,128]{4,3,2,1,0:T(8,128)S(1)}, f32[4,2,8,8,128]{4,3,2,1,0:T(8,128)S(1)}, u32[]{:S(2)}, u32[]{:S(2)}) collective-permute-start(f32[4,2,8,8,128]{4,3,2,1,0:T(8,128)S(1)} %get-tuple-element.10), channel_id=1, source_target_pairs={{0,1},{1,0},{2,3},{3,2},{4,5},{5,4},{6,7},{7,6},{8,9},{9,8},{10,11... | collective-permute-start | bytes 786440 | tf_op jit(solution)/shard_map/ppermute | solution.py:219
  7.8 8.7 %collective-permute-start.5 = (f32[2,8,8,128]{3,2,1,0:T(8,128)S(1)}, f32[2,8,8,128]{3,2,1,0:T(8,128)S(1)}, u32[]{:S(2)}, u32[]{:S(2)}) collective-permute-start(f32[2,8,8,128]{3,2,1,0:T(8,128)S(1)} %get-tuple-element.13), channel_id=1, source_target_pairs={{0,4},{4,8},{8,12},{12,0},{1,5},{5,9},{9,13},{13,1},{2,6},{6,10},{... | collective-permute-start | bytes 196616 | tf_op jit(solution)/shard_map/ppermute | solution.py:215
  9.5 7.4 %collective-permute-start.7 = (f32[2,8,8,128]{3,2,1,0:T(8,128)S(1)}, f32[2,8,8,128]{3,2,1,0:T(8,128)S(1)}, u32[]{:S(2)}, u32[]{:S(2)}) collective-permute-start(f32[2,8,8,128]{3,2,1,0:T(8,128)S(1)} %get-tuple-element.14), channel_id=1, source_target_pairs={{0,12},{4,0},{8,4},{12,8},{1,13},{5,1},{9,5},{13,9},{2,14},{6,2},{... | collective-permute-start | bytes 196616 | tf_op jit(solution)/shard_map/ppermute | solution.py:215
  11.1 6.0 %collective-permute-start.6 = (f32[2,8,8,128]{3,2,1,0:T(8,128)S(1)}, f32[2,8,8,128]{3,2,1,0:T(8,128)S(1)}, u32[]{:S(2)}, u32[]{:S(2)}) collective-permute-start(f32[2,8,8,128]{3,2,1,0:T(8,128)S(1)} %get-tuple-element.15), channel_id=1, source_target_pairs={{0,8},{4,12},{8,0},{12,4},{1,9},{5,13},{9,1},{13,5},{2,10},{6,14},... | collective-permute-start | bytes 196616 | tf_op jit(solution)/shard_map/ppermute | solution.py:215
  13.2 11.3 %collective-permute-start.1 = (f32[2,8,8,128]{3,2,1,0:T(8,128)S(1)}, f32[2,8,8,128]{3,2,1,0:T(8,128)S(1)}, u32[]{:S(2)}, u32[]{:S(2)}) collective-permute-start(f32[2,8,8,128]{3,2,1,0:T(8,128)S(1)} %get-tuple-element.16), channel_id=1, source_target_pairs={{0,4},{4,8},{8,12},{12,0},{1,5},{5,9},{9,13},{13,1},{2,6},{6,10},{... | collective-permute-start | bytes 196616 | tf_op jit(solution)/shard_map/ppermute | solution.py:215
  13.9 10.5 %collective-permute-start.3 = (f32[2,8,8,128]{3,2,1,0:T(8,128)S(1)}, f32[2,8,8,128]{3,2,1,0:T(8,128)S(1)}, u32[]{:S(2)}, u32[]{:S(2)}) collective-permute-start(f32[2,8,8,128]{3,2,1,0:T(8,128)S(1)} %get-tuple-element.17), channel_id=1, source_target_pairs={{0,12},{4,0},{8,4},{12,8},{1,13},{5,1},{9,5},{13,9},{2,14},{6,2},{... | collective-permute-start | bytes 196616 | tf_op jit(solution)/shard_map/ppermute | solution.py:215
  16.5 8.0 %collective-permute-start.2 = (f32[2,8,8,128]{3,2,1,0:T(8,128)S(1)}, f32[2,8,8,128]{3,2,1,0:T(8,128)S(1)}, u32[]{:S(2)}, u32[]{:S(2)}) collective-permute-start(f32[2,8,8,128]{3,2,1,0:T(8,128)S(1)} %get-tuple-element.18), channel_id=1, source_target_pairs={{0,8},{4,12},{8,0},{12,4},{1,9},{5,13},{9,1},{13,5},{2,10},{6,14},... | collective-permute-start | bytes 196616 | tf_op jit(solution)/shard_map/ppermute | solution.py:215
  17.2 9.6 %collective-permute-start.8 = (f32[2,8,8,128]{3,2,1,0:T(8,128)S(1)}, f32[2,8,8,128]{3,2,1,0:T(8,128)S(1)}, u32[]{:S(2)}, u32[]{:S(2)}) collective-permute-start(f32[2,8,8,128]{3,2,1,0:T(8,128)S(1)} %fusion.2), channel_id=1, source_target_pairs={{0,2},{2,0},{1,3},{3,1},{4,6},{6,4},{5,7},{7,5},{8,10},{10,8},{9,1... | collective-permute-start | bytes 196616 | tf_op jit(solution)/shard_map/ppermute | solution.py:219
  26.9 8.2 %collective-permute-start.13 = (f32[4,32,128]{2,1,0:T(8,128)S(1)}, f32[4,32,128]{2,1,0:T(8,128)S(1)}, u32[]{:S(2)}, u32[]{:S(2)}) collective-permute-start(f32[4,32,128]{2,1,0:T(8,128)S(1)} %turn.1.own_ref), channel_id=1, source_target_pairs={{0,48},{16,32},{32,16},{48,0},{1,49},{17,33},{33,17},{49,1},{2,50}... | collective-permute-start | bytes 196616 | tf_op jit(solution)/shard_map/ppermute | solution.py:219
  31.0 5.2 %collective-permute-start.12 = (f32[4,32,128]{2,1,0:T(8,128)S(1)}, f32[4,32,128]{2,1,0:T(8,128)S(1)}, u32[]{:S(2)}, u32[]{:S(2)}) collective-permute-start(f32[4,32,128]{2,1,0:T(8,128)S(1)} %turn.1.own_ref), channel_id=1, source_target_pairs={{0,32},{16,48},{32,0},{48,16},{1,33},{17,49},{33,1},{49,17},{2,34}... | collective-permute-start | bytes 196616 | tf_op jit(solution)/shard_map/ppermute | solution.py:219
  31.0 8.2 %collective-permute-start.11 = (f32[4,32,128]{2,1,0:T(8,128)S(1)}, f32[4,32,128]{2,1,0:T(8,128)S(1)}, u32[]{:S(2)}, u32[]{:S(2)}) collective-permute-start(f32[4,32,128]{2,1,0:T(8,128)S(1)} %turn.1.own_ref), channel_id=1, source_target_pairs={{0,192},{64,128},{128,64},{192,0},{1,193},{65,129},{129,65},{193,1... | collective-permute-start | bytes 196616 | tf_op jit(solution)/shard_map/ppermute | solution.py:219
  31.4 8.9 %collective-permute-start.10 = (f32[4,32,128]{2,1,0:T(8,128)S(1)}, f32[4,32,128]{2,1,0:T(8,128)S(1)}, u32[]{:S(2)}, u32[]{:S(2)}) collective-permute-start(f32[4,32,128]{2,1,0:T(8,128)S(1)} %turn.1.own_ref), channel_id=1, source_target_pairs={{0,128},{64,192},{128,0},{192,64},{1,129},{65,193},{129,1},{193,65... | collective-permute-start | bytes 196616 | tf_op jit(solution)/shard_map/ppermute | solution.py:219
  33.9 6.5 %collective-permute-start.9 = (f32[4,32,128]{2,1,0:T(8,128)S(1)}, f32[4,32,128]{2,1,0:T(8,128)S(1)}, u32[]{:S(2)}, u32[]{:S(2)}) collective-permute-start(f32[4,32,128]{2,1,0:T(8,128)S(1)} %turn.1.own_ref), channel_id=1, source_target_pairs={{0,64},{64,0},{128,192},{192,128},{1,65},{65,1},{129,193},{193,129... | collective-permute-start | bytes 196616 | tf_op jit(solution)/shard_map/ppermute | solution.py:219
  36.1 7.7 %collective-permute-start.17 = (f32[2,4,32,128]{3,2,1,0:T(8,128)S(1)}, f32[2,4,32,128]{3,2,1,0:T(8,128)S(1)}, u32[]{:S(2)}, u32[]{:S(2)}) collective-permute-start(f32[2,4,32,128]{3,2,1,0:T(8,128)S(1)} %pad_maximum_fusion.1), channel_id=1, source_target_pairs={{0,192},{64,128},{128,64},{192,0},{1,193},{65,129},{129,65},{193,1... | collective-permute-start | bytes 393224 | tf_op jit(solution)/shard_map/ppermute | solution.py:219
  36.7 7.1 %collective-permute-start.16 = (f32[2,4,32,128]{3,2,1,0:T(8,128)S(1)}, f32[2,4,32,128]{3,2,1,0:T(8,128)S(1)}, u32[]{:S(2)}, u32[]{:S(2)}) collective-permute-start(f32[2,4,32,128]{3,2,1,0:T(8,128)S(1)} %pad_maximum_fusion.1), channel_id=1, source_target_pairs={{0,128},{64,192},{128,0},{192,64},{1,129},{65,193},{129,1},{193,65... | collective-permute-start | bytes 393224 | tf_op jit(solution)/shard_map/ppermute | solution.py:219
  39.2 5.5 %collective-permute-start.15 = (f32[2,4,32,128]{3,2,1,0:T(8,128)S(1)}, f32[2,4,32,128]{3,2,1,0:T(8,128)S(1)}, u32[]{:S(2)}, u32[]{:S(2)}) collective-permute-start(f32[2,4,32,128]{3,2,1,0:T(8,128)S(1)} %pad_maximum_fusion.1), channel_id=1, source_target_pairs={{0,64},{64,0},{128,192},{192,128},{1,65},{65,1},{129,193},{193,129... | collective-permute-start | bytes 393224 | tf_op jit(solution)/shard_map/ppermute | solution.py:219
  40.4 6.5 %collective-permute-start.14 = (f32[4,4,32,128]{3,2,1,0:T(8,128)S(1)}, f32[4,4,32,128]{3,2,1,0:T(8,128)S(1)}, u32[]{:S(2)}, u32[]{:S(2)}) collective-permute-start(f32[4,4,32,128]{3,2,1,0:T(8,128)S(1)} %pad_maximum_fusion), channel_id=1, source_target_pairs={{0,16},{16,0},{32,48},{48,32},{1,17},{17,1},{33,49},{49,33},{2,18}... | collective-permute-start | bytes 786440 | tf_op jit(solution)/shard_map/ppermute | solution.py:219

commit v4 on v3

--- a/solution.py
+++ b/solution.py
@@ -234,7 +234,7 @@
 
 def summed_over_y(mine, other):
     summed = mine + swapped(other, "core", 1)
-    came = [shifted(summed[i], "y", i) for i in (1, 2, 3)]
+    came = [shifted(summed[i], "y", i) for i in (1, 3, 2)]
     return summed[0] + came[0] + came[1] + came[2]
 
 

time: 48.7 us -> 48.4 us (level)
    ppermute x12, starting transfers between devices: 20.2 us -> 19.6 us  [swapped(): lax.ppermute(array, axis, [(s, s ^ by) for s in range(lax.axis_size(axis))])]
  transfers between devices with their start and end apart: 18 -> 18, of which waited for: 7 -> 6; matrix products, arithmetic and copies ran while one was open for 0% -> 0% of each run, Pallas kernels for 0% -> 0%
where the time goes in v4:
time: 48.4 us; the launch traced here: 48.3 us
  starting transfers between devices  29 us (60%)
  waiting for transfers between devices  10.9 us (23%)
  Pallas kernels  7.96 us (16%)
    ppermute x12, starting transfers between devices, swapped(): lax.ppermute(array, axis, [(s, s ^ by) for s in range(lax.axis_size(axis))])  19.6 us
    ppermute x12, waiting for transfers between devices, swapped(): lax.ppermute(array, axis, [(s, s ^ by) for s in range(lax.axis_size(axis))])  10.9 us
    ppermute x6, starting transfers between devices, shifted(): lax.ppermute(array, axis, [(s, (s + by) % size) for s in range(size)])  9.43 us
    pallas_call x1, Pallas kernels, dft(): pl.pallas_call(dft_kernel, out_shape=(block,) * 4, in_specs=[SMEM, FAR, F...  6.02 us
    pallas_call x1, Pallas kernels, gram(): pl.pallas_call(functools.partial(gram_kernel, spots), out_shape=jax.Shape...  1.82 us
  transfers between devices with their start and end apart: 18, of which 6 were waited for; matrix products, arithmetic and copies ran while one was open for 0% of the time, Pallas kernels for 0%

profile of v4, /device:TPU:6, one launch (start us, length us, event | category | flops | bytes accessed | tf_op | source)
XLA Modules:
  0.0 48.3 jit_solution(1865875759074600464)
XLA Ops:
  0.0 0.1 stack.61.place
  0.1 6.0 %dft.1 = (f32[4,2,8,8,128]{4,3,2,1,0:T(8,128)S(1)}, f32[4,2,8,8,128]{4,3,2,1,0:T(8,128)S(1)}, f32[4,2,8,8,128]{4,3,2,1,0:T(8,128)S(1)}, f32[4,2,8,8,128]{4,3,2,1,0:T(8,128)S(1)}) custom-call(s32[6]{0:T(128)S(1)} %stack.61.place, s32[1,128]{1,0:T(1,128)} %bitcast.56, s32[1,128]{1,0:T(1,128)} %bitcast.57, bf16[4,2,4,8,32,640]{5,4,3,2,1,0:T(8,128)(2,1)} %bitcast.50), custom_call_target="tpu_custom_call" | custom-call | tf_op jit(solution)/shard_map/dft/pallas_call | solution.py:109
  6.1 0.1 collective-permute-start.4
  6.2 0.5 %collective-permute-start = (f32[4,2,8,8,128]{4,3,2,1,0:T(8,128)S(1)}, f32[4,2,8,8,128]{4,3,2,1,0:T(8,128)S(1)}, u32[]{:S(2)}, u32[]{:S(2)}) collective-permute-start(f32[4,2,8,8,128]{4,3,2,1,0:T(8,128)S(1)} %get-tuple-element.10), channel_id=1, source_target_pairs={{0,1},{1,0},{2,3},{3,2},{4,5},{5,4},{6,7},{7,6},{8,9},{9,8},{10,11... | collective-permute-start | bytes 786440 | tf_op jit(solution)/shard_map/ppermute | solution.py:219
  6.7 1.0 %collective-permute-done.4 = f32[4,2,8,8,128]{4,3,2,1,0:T(8,128)S(1)} collective-permute-done((f32[4,2,8,8,128]{4,3,2,1,0:T(8,128)S(1)}, f32[4,2,8,8,128]{4,3,2,1,0:T(8,128)S(1)}, u32[]{:S(2)}, u32[]{:S(2)}) %collective-permute-start.4) | collective-permute-done | bytes 262176 | tf_op jit(solution)/shard_map/ppermute | solution.py:219
  7.8 1.7 %collective-permute-start.5 = (f32[2,8,8,128]{3,2,1,0:T(8,128)S(1)}, f32[2,8,8,128]{3,2,1,0:T(8,128)S(1)}, u32[]{:S(2)}, u32[]{:S(2)}) collective-permute-start(f32[2,8,8,128]{3,2,1,0:T(8,128)S(1)} %get-tuple-element.13), channel_id=1, source_target_pairs={{0,4},{4,8},{8,12},{12,0},{1,5},{5,9},{9,13},{13,1},{2,6},{6,10},{... | collective-permute-start | bytes 196616 | tf_op jit(solution)/shard_map/ppermute | solution.py:215
  9.5 2.9 %collective-permute-start.7 = (f32[2,8,8,128]{3,2,1,0:T(8,128)S(1)}, f32[2,8,8,128]{3,2,1,0:T(8,128)S(1)}, u32[]{:S(2)}, u32[]{:S(2)}) collective-permute-start(f32[2,8,8,128]{3,2,1,0:T(8,128)S(1)} %get-tuple-element.14), channel_id=1, source_target_pairs={{0,8},{4,12},{8,0},{12,4},{1,9},{5,13},{9,1},{13,5},{2,10},{6,14},... | collective-permute-start | bytes 196616 | tf_op jit(solution)/shard_map/ppermute | solution.py:215
  12.4 1.3 %collective-permute-start.6 = (f32[2,8,8,128]{3,2,1,0:T(8,128)S(1)}, f32[2,8,8,128]{3,2,1,0:T(8,128)S(1)}, u32[]{:S(2)}, u32[]{:S(2)}) collective-permute-start(f32[2,8,8,128]{3,2,1,0:T(8,128)S(1)} %get-tuple-element.15), channel_id=1, source_target_pairs={{0,12},{4,0},{8,4},{12,8},{1,13},{5,1},{9,5},{13,9},{2,14},{6,2},{... | collective-permute-start | bytes 196616 | tf_op jit(solution)/shard_map/ppermute | solution.py:215
  13.7 0.0 collective-permute-done
  13.8 0.8 %collective-permute-start.1 = (f32[2,8,8,128]{3,2,1,0:T(8,128)S(1)}, f32[2,8,8,128]{3,2,1,0:T(8,128)S(1)}, u32[]{:S(2)}, u32[]{:S(2)}) collective-permute-start(f32[2,8,8,128]{3,2,1,0:T(8,128)S(1)} %get-tuple-element.16), channel_id=1, source_target_pairs={{0,4},{4,8},{8,12},{12,0},{1,5},{5,9},{9,13},{13,1},{2,6},{6,10},{... | collective-permute-start | bytes 196616 | tf_op jit(solution)/shard_map/ppermute | solution.py:215
  14.5 0.8 %collective-permute-start.3 = (f32[2,8,8,128]{3,2,1,0:T(8,128)S(1)}, f32[2,8,8,128]{3,2,1,0:T(8,128)S(1)}, u32[]{:S(2)}, u32[]{:S(2)}) collective-permute-start(f32[2,8,8,128]{3,2,1,0:T(8,128)S(1)} %get-tuple-element.17), channel_id=1, source_target_pairs={{0,8},{4,12},{8,0},{12,4},{1,9},{5,13},{9,1},{13,5},{2,10},{6,14},... | collective-permute-start | bytes 196616 | tf_op jit(solution)/shard_map/ppermute | solution.py:215
  15.3 0.0 collective-permute-done.5
  15.3 2.0 %collective-permute-start.2 = (f32[2,8,8,128]{3,2,1,0:T(8,128)S(1)}, f32[2,8,8,128]{3,2,1,0:T(8,128)S(1)}, u32[]{:S(2)}, u32[]{:S(2)}) collective-permute-start(f32[2,8,8,128]{3,2,1,0:T(8,128)S(1)} %get-tuple-element.18), channel_id=1, source_target_pairs={{0,12},{4,0},{8,4},{12,8},{1,13},{5,1},{9,5},{13,9},{2,14},{6,2},{... | collective-permute-start | bytes 196616 | tf_op jit(solution)/shard_map/ppermute | solution.py:215
  17.3 0.0 collective-permute-done.7
  17.3 0.0 collective-permute-done.6
  17.3 7.3 %collective-permute-start.8 = (f32[2,8,8,128]{3,2,1,0:T(8,128)S(1)}, f32[2,8,8,128]{3,2,1,0:T(8,128)S(1)}, u32[]{:S(2)}, u32[]{:S(2)}) collective-permute-start(f32[2,8,8,128]{3,2,1,0:T(8,128)S(1)} %fusion.2), channel_id=1, source_target_pairs={{0,2},{2,0},{1,3},{3,1},{4,6},{6,4},{5,7},{7,5},{8,10},{10,8},{9,1... | collective-permute-start | bytes 196616 | tf_op jit(solution)/shard_map/ppermute | solution.py:219
  24.6 0.0 collective-permute-done.1
  24.6 0.0 collective-permute-done.3
  24.6 0.0 collective-permute-done.2
  24.6 2.3 %collective-permute-done.8.came_ref = f32[2,8,8,128]{3,2,1,0:T(8,128)S(1)} collective-permute-done((f32[2,8,8,128]{3,2,1,0:T(8,128)S(1)}, f32[2,8,8,128]{3,2,1,0:T(8,128)S(1)}, u32[]{:S(2)}, u32[]{:S(2)}) %collective-permute-start.8) | collective-permute-done | bytes 65568 | tf_op jit(solution)/shard_map/ppermute | solution.py:219
  26.9 0.1 turn.1.own_ref
  27.1 3.3 %collective-permute-start.13 = (f32[4,32,128]{2,1,0:T(8,128)S(1)}, f32[4,32,128]{2,1,0:T(8,128)S(1)}, u32[]{:S(2)}, u32[]{:S(2)}) collective-permute-start(f32[4,32,128]{2,1,0:T(8,128)S(1)} %turn.1.own_ref), channel_id=1, source_target_pairs={{0,48},{16,32},{32,16},{48,0},{1,49},{17,33},{33,17},{49,1},{2,50}... | collective-permute-start | bytes 196616 | tf_op jit(solution)/shard_map/ppermute | solution.py:219
  30.4 0.0 collective-permute-start.12
  30.4 0.5 collective-permute-start.11
  30.9 2.4 %collective-permute-start.10 = (f32[4,32,128]{2,1,0:T(8,128)S(1)}, f32[4,32,128]{2,1,0:T(8,128)S(1)}, u32[]{:S(2)}, u32[]{:S(2)}) collective-permute-start(f32[4,32,128]{2,1,0:T(8,128)S(1)} %turn.1.own_ref), channel_id=1, source_target_pairs={{0,128},{64,192},{128,0},{192,64},{1,129},{65,193},{129,1},{193,65... | collective-permute-start | bytes 196616 | tf_op jit(solution)/shard_map/ppermute | solution.py:219
  33.3 1.2 %collective-permute-start.9 = (f32[4,32,128]{2,1,0:T(8,128)S(1)}, f32[4,32,128]{2,1,0:T(8,128)S(1)}, u32[]{:S(2)}, u32[]{:S(2)}) collective-permute-start(f32[4,32,128]{2,1,0:T(8,128)S(1)} %turn.1.own_ref), channel_id=1, source_target_pairs={{0,64},{64,0},{128,192},{192,128},{1,65},{65,1},{129,193},{193,129... | collective-permute-start | bytes 196616 | tf_op jit(solution)/shard_map/ppermute | solution.py:219
  34.5 0.0 collective-permute-done.13
  34.5 1.2 %collective-permute-done.12 = f32[4,32,128]{2,1,0:T(8,128)S(1)} collective-permute-done((f32[4,32,128]{2,1,0:T(8,128)S(1)}, f32[4,32,128]{2,1,0:T(8,128)S(1)}, u32[]{:S(2)}, u32[]{:S(2)}) %collective-permute-start.12) | collective-permute-done | bytes 65568 | tf_op jit(solution)/shard_map/ppermute | solution.py:219
  35.8 0.6 %collective-permute-start.17 = (f32[2,4,32,128]{3,2,1,0:T(8,128)S(1)}, f32[2,4,32,128]{3,2,1,0:T(8,128)S(1)}, u32[]{:S(2)}, u32[]{:S(2)}) collective-permute-start(f32[2,4,32,128]{3,2,1,0:T(8,128)S(1)} %pad_maximum_fusion.1), channel_id=1, source_target_pairs={{0,192},{64,128},{128,64},{192,0},{1,193},{65,129},{129,65},{193,1... | collective-permute-start | bytes 393224 | tf_op jit(solution)/shard_map/ppermute | solution.py:219
  36.4 2.4 %collective-permute-start.16 = (f32[2,4,32,128]{3,2,1,0:T(8,128)S(1)}, f32[2,4,32,128]{3,2,1,0:T(8,128)S(1)}, u32[]{:S(2)}, u32[]{:S(2)}) collective-permute-start(f32[2,4,32,128]{3,2,1,0:T(8,128)S(1)} %pad_maximum_fusion.1), channel_id=1, source_target_pairs={{0,128},{64,192},{128,0},{192,64},{1,129},{65,193},{129,1},{193,65... | collective-permute-start | bytes 393224 | tf_op jit(solution)/shard_map/ppermute | solution.py:219
  38.8 0.0 collective-permute-done.11
  38.8 1.2 %collective-permute-start.15 = (f32[2,4,32,128]{3,2,1,0:T(8,128)S(1)}, f32[2,4,32,128]{3,2,1,0:T(8,128)S(1)}, u32[]{:S(2)}, u32[]{:S(2)}) collective-permute-start(f32[2,4,32,128]{3,2,1,0:T(8,128)S(1)} %pad_maximum_fusion.1), channel_id=1, source_target_pairs={{0,64},{64,0},{128,192},{192,128},{1,65},{65,1},{129,193},{193,129... | collective-permute-start | bytes 393224 | tf_op jit(solution)/shard_map/ppermute | solution.py:219
  40.0 0.0 collective-permute-done.10
  40.0 0.0 collective-permute-done.9
  40.0 0.1 collective-permute-start.14
  40.2 3.3 %collective-permute-done.17.refs_4_ = f32[2,4,32,128]{3,2,1,0:T(8,128)S(1)} collective-permute-done((f32[2,4,32,128]{3,2,1,0:T(8,128)S(1)}, f32[2,4,32,128]{3,2,1,0:T(8,128)S(1)}, u32[]{:S(2)}, u32[]{:S(2)}) %collective-permute-start.17) | collective-permute-done | bytes 131104 | tf_op jit(solution)/shard_map/ppermute | solution.py:219
  43.5 0.0 collective-permute-done.16.refs_3_
  43.5 0.9 %collective-permute-done.15.refs_2_ = f32[2,4,32,128]{3,2,1,0:T(8,128)S(1)} collective-permute-done((f32[2,4,32,128]{3,2,1,0:T(8,128)S(1)}, f32[2,4,32,128]{3,2,1,0:T(8,128)S(1)}, u32[]{:S(2)}, u32[]{:S(2)}) %collective-permute-start.15) | collective-permute-done | bytes 131104 | tf_op jit(solution)/shard_map/ppermute | solution.py:219
  44.3 2.1 %collective-permute-done.14.refs_1_ = f32[4,4,32,128]{3,2,1,0:T(8,128)S(1)} collective-permute-done((f32[4,4,32,128]{3,2,1,0:T(8,128)S(1)}, f32[4,4,32,128]{3,2,1,0:T(8,128)S(1)}, u32[]{:S(2)}, u32[]{:S(2)}) %collective-permute-start.14) | collective-permute-done | bytes 262176 | tf_op jit(solution)/shard_map/ppermute | solution.py:219
  46.5 1.8 %gram.1 = f32[2,8,32,512]{3,2,1,0:T(8,128)} custom-call(s32[6]{0:T(128)S(1)} %stack.61.place, f32[4,32,128]{2,1,0:T(8,128)S(1)} %turn.1.own_ref, f32[6,4,32,128]{3,2,1,0:T(8,128)S(1)} %constant_dynamic-update-slice_fusion.refs_0_, f32[4,4,32,128]{3,2,1,0:T(8,128)S(1)} %collective-permute-done.14.refs_1_, ...), custom_call_target="tpu_custom_call" | custom-call | tf_op jit(solution)/shard_map/gram/pallas_call | solution.py:198
  (14 shorter events, 0.2 us)
Async XLA Ops:
  6.1 1.6 %collective-permute-start.4 = (f32[4,2,8,8,128]{4,3,2,1,0:T(8,128)S(1)}, f32[4,2,8,8,128]{4,3,2,1,0:T(8,128)S(1)}, u32[]{:S(2)}, u32[]{:S(2)}) collective-permute-start(f32[4,2,8,8,128]{4,3,2,1,0:T(8,128)S(1)} %get-tuple-element.12), channel_id=1, source_target_pairs={{0,1},{1,0},{2,3},{3,2},{4,5},{5,4},{6,7},{7,6},{8,9},{9,8},{10,11... | collective-permute-start | bytes 786440 | tf_op jit(solution)/shard_map/ppermute | solution.py:219
  6.2 7.5 %collective-permute-start = (f32[4,2,8,8,128]{4,3,2,1,0:T(8,128)S(1)}, f32[4,2,8,8,128]{4,3,2,1,0:T(8,128)S(1)}, u32[]{:S(2)}, u32[]{:S(2)}) collective-permute-start(f32[4,2,8,8,128]{4,3,2,1,0:T(8,128)S(1)} %get-tuple-element.10), channel_id=1, source_target_pairs={{0,1},{1,0},{2,3},{3,2},{4,5},{5,4},{6,7},{7,6},{8,9},{9,8},{10,11... | collective-permute-start | bytes 786440 | tf_op jit(solution)/shard_map/ppermute | solution.py:219
  7.8 7.5 %collective-permute-start.5 = (f32[2,8,8,128]{3,2,1,0:T(8,128)S(1)}, f32[2,8,8,128]{3,2,1,0:T(8,128)S(1)}, u32[]{:S(2)}, u32[]{:S(2)}) collective-permute-start(f32[2,8,8,128]{3,2,1,0:T(8,128)S(1)} %get-tuple-element.13), channel_id=1, source_target_pairs={{0,4},{4,8},{8,12},{12,0},{1,5},{5,9},{9,13},{13,1},{2,6},{6,10},{... | collective-permute-start | bytes 196616 | tf_op jit(solution)/shard_map/ppermute | solution.py:215
  9.5 7.8 %collective-permute-start.7 = (f32[2,8,8,128]{3,2,1,0:T(8,128)S(1)}, f32[2,8,8,128]{3,2,1,0:T(8,128)S(1)}, u32[]{:S(2)}, u32[]{:S(2)}) collective-permute-start(f32[2,8,8,128]{3,2,1,0:T(8,128)S(1)} %get-tuple-element.14), channel_id=1, source_target_pairs={{0,8},{4,12},{8,0},{12,4},{1,9},{5,13},{9,1},{13,5},{2,10},{6,14},... | collective-permute-start | bytes 196616 | tf_op jit(solution)/shard_map/ppermute | solution.py:215
  12.4 4.9 %collective-permute-start.6 = (f32[2,8,8,128]{3,2,1,0:T(8,128)S(1)}, f32[2,8,8,128]{3,2,1,0:T(8,128)S(1)}, u32[]{:S(2)}, u32[]{:S(2)}) collective-permute-start(f32[2,8,8,128]{3,2,1,0:T(8,128)S(1)} %get-tuple-element.15), channel_id=1, source_target_pairs={{0,12},{4,0},{8,4},{12,8},{1,13},{5,1},{9,5},{13,9},{2,14},{6,2},{... | collective-permute-start | bytes 196616 | tf_op jit(solution)/shard_map/ppermute | solution.py:215
  13.8 10.8 %collective-permute-start.1 = (f32[2,8,8,128]{3,2,1,0:T(8,128)S(1)}, f32[2,8,8,128]{3,2,1,0:T(8,128)S(1)}, u32[]{:S(2)}, u32[]{:S(2)}) collective-permute-start(f32[2,8,8,128]{3,2,1,0:T(8,128)S(1)} %get-tuple-element.16), channel_id=1, source_target_pairs={{0,4},{4,8},{8,12},{12,0},{1,5},{5,9},{9,13},{13,1},{2,6},{6,10},{... | collective-permute-start | bytes 196616 | tf_op jit(solution)/shard_map/ppermute | solution.py:215
  14.5 10.1 %collective-permute-start.3 = (f32[2,8,8,128]{3,2,1,0:T(8,128)S(1)}, f32[2,8,8,128]{3,2,1,0:T(8,128)S(1)}, u32[]{:S(2)}, u32[]{:S(2)}) collective-permute-start(f32[2,8,8,128]{3,2,1,0:T(8,128)S(1)} %get-tuple-element.17), channel_id=1, source_target_pairs={{0,8},{4,12},{8,0},{12,4},{1,9},{5,13},{9,1},{13,5},{2,10},{6,14},... | collective-permute-start | bytes 196616 | tf_op jit(solution)/shard_map/ppermute | solution.py:215
  15.3 9.3 %collective-permute-start.2 = (f32[2,8,8,128]{3,2,1,0:T(8,128)S(1)}, f32[2,8,8,128]{3,2,1,0:T(8,128)S(1)}, u32[]{:S(2)}, u32[]{:S(2)}) collective-permute-start(f32[2,8,8,128]{3,2,1,0:T(8,128)S(1)} %get-tuple-element.18), channel_id=1, source_target_pairs={{0,12},{4,0},{8,4},{12,8},{1,13},{5,1},{9,5},{13,9},{2,14},{6,2},{... | collective-permute-start | bytes 196616 | tf_op jit(solution)/shard_map/ppermute | solution.py:215
  17.3 9.6 %collective-permute-start.8 = (f32[2,8,8,128]{3,2,1,0:T(8,128)S(1)}, f32[2,8,8,128]{3,2,1,0:T(8,128)S(1)}, u32[]{:S(2)}, u32[]{:S(2)}) collective-permute-start(f32[2,8,8,128]{3,2,1,0:T(8,128)S(1)} %fusion.2), channel_id=1, source_target_pairs={{0,2},{2,0},{1,3},{3,1},{4,6},{6,4},{5,7},{7,5},{8,10},{10,8},{9,1... | collective-permute-start | bytes 196616 | tf_op jit(solution)/shard_map/ppermute | solution.py:219
  27.1 7.5 %collective-permute-start.13 = (f32[4,32,128]{2,1,0:T(8,128)S(1)}, f32[4,32,128]{2,1,0:T(8,128)S(1)}, u32[]{:S(2)}, u32[]{:S(2)}) collective-permute-start(f32[4,32,128]{2,1,0:T(8,128)S(1)} %turn.1.own_ref), channel_id=1, source_target_pairs={{0,48},{16,32},{32,16},{48,0},{1,49},{17,33},{33,17},{49,1},{2,50}... | collective-permute-start | bytes 196616 | tf_op jit(solution)/shard_map/ppermute | solution.py:219
  30.4 5.4 %collective-permute-start.12 = (f32[4,32,128]{2,1,0:T(8,128)S(1)}, f32[4,32,128]{2,1,0:T(8,128)S(1)}, u32[]{:S(2)}, u32[]{:S(2)}) collective-permute-start(f32[4,32,128]{2,1,0:T(8,128)S(1)} %turn.1.own_ref), channel_id=1, source_target_pairs={{0,32},{16,48},{32,0},{48,16},{1,33},{17,49},{33,1},{49,17},{2,34}... | collective-permute-start | bytes 196616 | tf_op jit(solution)/shard_map/ppermute | solution.py:219
  30.4 8.4 %collective-permute-start.11 = (f32[4,32,128]{2,1,0:T(8,128)S(1)}, f32[4,32,128]{2,1,0:T(8,128)S(1)}, u32[]{:S(2)}, u32[]{:S(2)}) collective-permute-start(f32[4,32,128]{2,1,0:T(8,128)S(1)} %turn.1.own_ref), channel_id=1, source_target_pairs={{0,192},{64,128},{128,64},{192,0},{1,193},{65,129},{129,65},{193,1... | collective-permute-start | bytes 196616 | tf_op jit(solution)/shard_map/ppermute | solution.py:219
  30.9 9.1 %collective-permute-start.10 = (f32[4,32,128]{2,1,0:T(8,128)S(1)}, f32[4,32,128]{2,1,0:T(8,128)S(1)}, u32[]{:S(2)}, u32[]{:S(2)}) collective-permute-start(f32[4,32,128]{2,1,0:T(8,128)S(1)} %turn.1.own_ref), channel_id=1, source_target_pairs={{0,128},{64,192},{128,0},{192,64},{1,129},{65,193},{129,1},{193,65... | collective-permute-start | bytes 196616 | tf_op jit(solution)/shard_map/ppermute | solution.py:219
  33.3 6.7 %collective-permute-start.9 = (f32[4,32,128]{2,1,0:T(8,128)S(1)}, f32[4,32,128]{2,1,0:T(8,128)S(1)}, u32[]{:S(2)}, u32[]{:S(2)}) collective-permute-start(f32[4,32,128]{2,1,0:T(8,128)S(1)} %turn.1.own_ref), channel_id=1, source_target_pairs={{0,64},{64,0},{128,192},{192,128},{1,65},{65,1},{129,193},{193,129... | collective-permute-start | bytes 196616 | tf_op jit(solution)/shard_map/ppermute | solution.py:219
  35.8 7.7 %collective-permute-start.17 = (f32[2,4,32,128]{3,2,1,0:T(8,128)S(1)}, f32[2,4,32,128]{3,2,1,0:T(8,128)S(1)}, u32[]{:S(2)}, u32[]{:S(2)}) collective-permute-start(f32[2,4,32,128]{3,2,1,0:T(8,128)S(1)} %pad_maximum_fusion.1), channel_id=1, source_target_pairs={{0,192},{64,128},{128,64},{192,0},{1,193},{65,129},{129,65},{193,1... | collective-permute-start | bytes 393224 | tf_op jit(solution)/shard_map/ppermute | solution.py:219
  36.4 7.1 %collective-permute-start.16 = (f32[2,4,32,128]{3,2,1,0:T(8,128)S(1)}, f32[2,4,32,128]{3,2,1,0:T(8,128)S(1)}, u32[]{:S(2)}, u32[]{:S(2)}) collective-permute-start(f32[2,4,32,128]{3,2,1,0:T(8,128)S(1)} %pad_maximum_fusion.1), channel_id=1, source_target_pairs={{0,128},{64,192},{128,0},{192,64},{1,129},{65,193},{129,1},{193,65... | collective-permute-start | bytes 393224 | tf_op jit(solution)/shard_map/ppermute | solution.py:219
  38.8 5.5 %collective-permute-start.15 = (f32[2,4,32,128]{3,2,1,0:T(8,128)S(1)}, f32[2,4,32,128]{3,2,1,0:T(8,128)S(1)}, u32[]{:S(2)}, u32[]{:S(2)}) collective-permute-start(f32[2,4,32,128]{3,2,1,0:T(8,128)S(1)} %pad_maximum_fusion.1), channel_id=1, source_target_pairs={{0,64},{64,0},{128,192},{192,128},{1,65},{65,1},{129,193},{193,129... | collective-permute-start | bytes 393224 | tf_op jit(solution)/shard_map/ppermute | solution.py:219
  40.0 6.5 %collective-permute-start.14 = (f32[4,4,32,128]{3,2,1,0:T(8,128)S(1)}, f32[4,4,32,128]{3,2,1,0:T(8,128)S(1)}, u32[]{:S(2)}, u32[]{:S(2)}) collective-permute-start(f32[4,4,32,128]{3,2,1,0:T(8,128)S(1)} %pad_maximum_fusion), channel_id=1, source_target_pairs={{0,16},{16,0},{32,48},{48,32},{1,17},{17,1},{33,49},{49,33},{2,18}... | collective-permute-start | bytes 786440 | tf_op jit(solution)/shard_map/ppermute | solution.py:219

commit v5 on v4

--- a/solution.py
+++ b/solution.py
@@ -161,16 +161,18 @@
     return lax.dot_general(left, right, (((1,), (1,)), ((), ())), preferred_element_type=jnp.float32)
 
 
-def gram_kernel(spots, place, own_ref, *refs):
-    blocks, (out_hbm, right, out, sems) = refs[:-4], refs[-4:]
+def place_blocks(place, blocks, spots, kk, right):
     x, zl = place[4], place[5]
+    for block, group in zip(blocks, spots):
+        for n, (i, j) in enumerate(group):
+            at = pl.multiple_of(((x ^ i) * 4 + (zl ^ j)) * 32, 32)
+            right[kk, pl.ds(at, 32), :] = block[n, kk].astype(jnp.bfloat16)
+
+
+def prepare_kernel(spots, place, own_ref, block, left_ref, right):
     lane = lax.broadcasted_iota(jnp.int32, (32, 128), 1) // 32
-    copies = []
     for kk in range(4):
-        for block, group in zip(blocks, spots):
-            for n, (i, j) in enumerate(group):
-                at = pl.multiple_of(((x ^ i) * 4 + (zl ^ j)) * 32, 32)
-                right[kk, pl.ds(at, 32), :] = block[n, kk].astype(jnp.bfloat16)
+        place_blocks(place, [block], spots, kk, right)
         own = own_ref[kk] * (1.0 / 32)
         turned = jnp.where(lane % 2 == 0, pltpu.roll(own, 96, 1), -pltpu.roll(own, 32, 1))
         left = []
@@ -181,7 +183,15 @@
         whole = jnp.concatenate(left, axis=0)
         high = whole.astype(jnp.bfloat16)
         low = (whole - high.astype(jnp.float32)).astype(jnp.bfloat16)
-        product = against(jnp.concatenate([high, low], axis=1), jnp.concatenate([right[kk], right[kk]], axis=1))
+        left_ref[kk] = jnp.concatenate([high, low], axis=1)
+
+
+def gram_kernel(spots, place, left_ref, right_in, *refs):
+    blocks, (out_hbm, right, out, sems) = refs[:-4], refs[-4:]
+    copies = []
+    for kk in range(4):
+        place_blocks(place, blocks, spots, kk, right)
+        product = against(left_ref[kk], jnp.concatenate([right[kk], right[kk]], axis=1))
         for k2 in range(2):
             for c in range(2):
                 base = (k2 * 2 + c) * 32
@@ -195,19 +205,25 @@
 
 def gram(place, own, blocks, spots):
     shape = (2, 8, 32, 512)
+    right_shape = jax.ShapeDtypeStruct((4, 512, 128), jnp.bfloat16)
+    left, right = pl.pallas_call(
+        functools.partial(prepare_kernel, spots[:1]),
+        out_shape=(jax.ShapeDtypeStruct((4, 128, 256), jnp.bfloat16), right_shape),
+        in_specs=[SMEM, VMEM, VMEM],
+        out_specs=(VMEM, VMEM),
+        compiler_params=PARAMS,
+        name="prepare",
+    )(place, own, blocks[0])
     return pl.pallas_call(
-        functools.partial(gram_kernel, spots),
-        out_shape=jax.ShapeDtypeStruct(shape, jnp.float32),
-        in_specs=[SMEM, VMEM] + [VMEM] * len(blocks),
-        out_specs=HBM,
-        scratch_shapes=[
-            pltpu.VMEM((4, 512, 128), jnp.bfloat16),
-            pltpu.VMEM(shape, jnp.float32),
-            pltpu.SemaphoreType.DMA((4,)),
-        ],
+        functools.partial(gram_kernel, spots[1:]),
+        out_shape=(jax.ShapeDtypeStruct(shape, jnp.float32), right_shape),
+        in_specs=[SMEM] + [VMEM] * (1 + len(blocks)),
+        out_specs=(HBM, VMEM),
+        input_output_aliases={2: 1},
+        scratch_shapes=[pltpu.VMEM(shape, jnp.float32), pltpu.SemaphoreType.DMA((4,))],
         compiler_params=PARAMS,
         name="gram",
-    )(place, own, *blocks)
+    )(place, left, right, *blocks[1:])[0]
 
 
 def shifted(array, axis, by):

time: 48.4 us -> 48.4 us (level)
  waiting for transfers between devices: 10.9 us -> 10.2 us
  Pallas kernels: 7.96 us -> 8.6 us
    ppermute x12, waiting for transfers between devices: 10.9 us -> 10.2 us  [swapped(): lax.ppermute(array, axis, [(s, s ^ by) for s in range(lax.axis_size(axis))])]
    pallas_call x1 -> x2, Pallas kernels: 1.82 us -> 2.45 us  [the longest x1 1.8 us: gram(): pl.pallas_call(functools.partial(gram_kernel, spots[1:]), out_shape=(jax....]
  transfers between devices with their start and end apart: 18 -> 18, of which waited for: 6 -> 6; matrix products, arithmetic and copies ran while one was open for 0% -> 0% of each run, Pallas kernels for 0% -> 1%
where the time goes in v5:
time: 48.4 us; the launch traced here: 48.3 us
  starting transfers between devices  29 us (60%)
  waiting for transfers between devices  10.2 us (21%)
  Pallas kernels  8.6 us (18%)
    ppermute x12, starting transfers between devices, swapped(): lax.ppermute(array, axis, [(s, s ^ by) for s in range(lax.axis_size(axis))])  19.6 us
    ppermute x12, waiting for transfers between devices, swapped(): lax.ppermute(array, axis, [(s, s ^ by) for s in range(lax.axis_size(axis))])  10.2 us
    ppermute x6, starting transfers between devices, shifted(): lax.ppermute(array, axis, [(s, (s + by) % size) for s in range(size)])  9.43 us
    pallas_call x1, Pallas kernels, dft(): pl.pallas_call(dft_kernel, out_shape=(block,) * 4, in_specs=[SMEM, FAR, F...  6.02 us
    pallas_call x1, Pallas kernels, gram(): pl.pallas_call(functools.partial(gram_kernel, spots[1:]), out_shape=(jax....  1.8 us
  transfers between devices with their start and end apart: 18, of which 6 were waited for; matrix products, arithmetic and copies ran while one was open for 0% of the time, Pallas kernels for 1%

profile of v5, /device:TPU:6, one launch (start us, length us, event | category | flops | bytes accessed | tf_op | source)
XLA Modules:
  0.0 48.3 jit_solution(16964772604831345577)
XLA Ops:
  0.0 0.1 stack.61.place
  0.1 6.0 %dft.1 = (f32[4,2,8,8,128]{4,3,2,1,0:T(8,128)S(1)}, f32[4,2,8,8,128]{4,3,2,1,0:T(8,128)S(1)}, f32[4,2,8,8,128]{4,3,2,1,0:T(8,128)S(1)}, f32[4,2,8,8,128]{4,3,2,1,0:T(8,128)S(1)}) custom-call(s32[6]{0:T(128)S(1)} %stack.61.place, s32[1,128]{1,0:T(1,128)} %bitcast.56, s32[1,128]{1,0:T(1,128)} %bitcast.57, bf16[4,2,4,8,32,640]{5,4,3,2,1,0:T(8,128)(2,1)} %bitcast.50), custom_call_target="tpu_custom_call" | custom-call | tf_op jit(solution)/shard_map/dft/pallas_call | solution.py:109
  6.1 0.1 collective-permute-start.4
  6.2 0.5 %collective-permute-start = (f32[4,2,8,8,128]{4,3,2,1,0:T(8,128)S(1)}, f32[4,2,8,8,128]{4,3,2,1,0:T(8,128)S(1)}, u32[]{:S(2)}, u32[]{:S(2)}) collective-permute-start(f32[4,2,8,8,128]{4,3,2,1,0:T(8,128)S(1)} %get-tuple-element.13), channel_id=1, source_target_pairs={{0,1},{1,0},{2,3},{3,2},{4,5},{5,4},{6,7},{7,6},{8,9},{9,8},{10,11... | collective-permute-start | bytes 786440 | tf_op jit(solution)/shard_map/ppermute | solution.py:235
  6.7 1.0 %collective-permute-done.4 = f32[4,2,8,8,128]{4,3,2,1,0:T(8,128)S(1)} collective-permute-done((f32[4,2,8,8,128]{4,3,2,1,0:T(8,128)S(1)}, f32[4,2,8,8,128]{4,3,2,1,0:T(8,128)S(1)}, u32[]{:S(2)}, u32[]{:S(2)}) %collective-permute-start.4) | collective-permute-done | bytes 262176 | tf_op jit(solution)/shard_map/ppermute | solution.py:235
  7.8 1.7 %collective-permute-start.5 = (f32[2,8,8,128]{3,2,1,0:T(8,128)S(1)}, f32[2,8,8,128]{3,2,1,0:T(8,128)S(1)}, u32[]{:S(2)}, u32[]{:S(2)}) collective-permute-start(f32[2,8,8,128]{3,2,1,0:T(8,128)S(1)} %get-tuple-element.19), channel_id=1, source_target_pairs={{0,4},{4,8},{8,12},{12,0},{1,5},{5,9},{9,13},{13,1},{2,6},{6,10},{... | collective-permute-start | bytes 196616 | tf_op jit(solution)/shard_map/ppermute | solution.py:231
  9.5 2.9 %collective-permute-start.7 = (f32[2,8,8,128]{3,2,1,0:T(8,128)S(1)}, f32[2,8,8,128]{3,2,1,0:T(8,128)S(1)}, u32[]{:S(2)}, u32[]{:S(2)}) collective-permute-start(f32[2,8,8,128]{3,2,1,0:T(8,128)S(1)} %get-tuple-element.20), channel_id=1, source_target_pairs={{0,8},{4,12},{8,0},{12,4},{1,9},{5,13},{9,1},{13,5},{2,10},{6,14},... | collective-permute-start | bytes 196616 | tf_op jit(solution)/shard_map/ppermute | solution.py:231
  12.4 1.3 %collective-permute-start.6 = (f32[2,8,8,128]{3,2,1,0:T(8,128)S(1)}, f32[2,8,8,128]{3,2,1,0:T(8,128)S(1)}, u32[]{:S(2)}, u32[]{:S(2)}) collective-permute-start(f32[2,8,8,128]{3,2,1,0:T(8,128)S(1)} %get-tuple-element.21), channel_id=1, source_target_pairs={{0,12},{4,0},{8,4},{12,8},{1,13},{5,1},{9,5},{13,9},{2,14},{6,2},{... | collective-permute-start | bytes 196616 | tf_op jit(solution)/shard_map/ppermute | solution.py:231
  13.7 0.0 collective-permute-done
  13.8 0.8 %collective-permute-start.1 = (f32[2,8,8,128]{3,2,1,0:T(8,128)S(1)}, f32[2,8,8,128]{3,2,1,0:T(8,128)S(1)}, u32[]{:S(2)}, u32[]{:S(2)}) collective-permute-start(f32[2,8,8,128]{3,2,1,0:T(8,128)S(1)} %get-tuple-element.22), channel_id=1, source_target_pairs={{0,4},{4,8},{8,12},{12,0},{1,5},{5,9},{9,13},{13,1},{2,6},{6,10},{... | collective-permute-start | bytes 196616 | tf_op jit(solution)/shard_map/ppermute | solution.py:231
  14.5 0.8 %collective-permute-start.3 = (f32[2,8,8,128]{3,2,1,0:T(8,128)S(1)}, f32[2,8,8,128]{3,2,1,0:T(8,128)S(1)}, u32[]{:S(2)}, u32[]{:S(2)}) collective-permute-start(f32[2,8,8,128]{3,2,1,0:T(8,128)S(1)} %get-tuple-element.23), channel_id=1, source_target_pairs={{0,8},{4,12},{8,0},{12,4},{1,9},{5,13},{9,1},{13,5},{2,10},{6,14},... | collective-permute-start | bytes 196616 | tf_op jit(solution)/shard_map/ppermute | solution.py:231
  15.3 0.0 collective-permute-done.5
  15.3 2.0 %collective-permute-start.2 = (f32[2,8,8,128]{3,2,1,0:T(8,128)S(1)}, f32[2,8,8,128]{3,2,1,0:T(8,128)S(1)}, u32[]{:S(2)}, u32[]{:S(2)}) collective-permute-start(f32[2,8,8,128]{3,2,1,0:T(8,128)S(1)} %get-tuple-element.24), channel_id=1, source_target_pairs={{0,12},{4,0},{8,4},{12,8},{1,13},{5,1},{9,5},{13,9},{2,14},{6,2},{... | collective-permute-start | bytes 196616 | tf_op jit(solution)/shard_map/ppermute | solution.py:231
  17.3 0.0 collective-permute-done.7
  17.3 0.0 collective-permute-done.6
  17.3 7.3 %collective-permute-start.8 = (f32[2,8,8,128]{3,2,1,0:T(8,128)S(1)}, f32[2,8,8,128]{3,2,1,0:T(8,128)S(1)}, u32[]{:S(2)}, u32[]{:S(2)}) collective-permute-start(f32[2,8,8,128]{3,2,1,0:T(8,128)S(1)} %fusion.2), channel_id=1, source_target_pairs={{0,2},{2,0},{1,3},{3,1},{4,6},{6,4},{5,7},{7,5},{8,10},{10,8},{9,1... | collective-permute-start | bytes 196616 | tf_op jit(solution)/shard_map/ppermute | solution.py:235
  24.6 0.0 collective-permute-done.1
  24.6 0.0 collective-permute-done.3
  24.6 0.0 collective-permute-done.2
  24.6 2.3 %collective-permute-done.8.came_ref = f32[2,8,8,128]{3,2,1,0:T(8,128)S(1)} collective-permute-done((f32[2,8,8,128]{3,2,1,0:T(8,128)S(1)}, f32[2,8,8,128]{3,2,1,0:T(8,128)S(1)}, u32[]{:S(2)}, u32[]{:S(2)}) %collective-permute-start.8) | collective-permute-done | bytes 65568 | tf_op jit(solution)/shard_map/ppermute | solution.py:235
  26.9 0.1 turn.1.own_ref
  27.1 3.3 %collective-permute-start.13 = (f32[4,32,128]{2,1,0:T(8,128)S(1)}, f32[4,32,128]{2,1,0:T(8,128)S(1)}, u32[]{:S(2)}, u32[]{:S(2)}) collective-permute-start(f32[4,32,128]{2,1,0:T(8,128)S(1)} %turn.1.own_ref), channel_id=1, source_target_pairs={{0,48},{16,32},{32,16},{48,0},{1,49},{17,33},{33,17},{49,1},{2,50}... | collective-permute-start | bytes 196616 | tf_op jit(solution)/shard_map/ppermute | solution.py:235
  30.4 0.0 collective-permute-start.12
  30.4 0.5 collective-permute-start.11
  30.9 2.4 %collective-permute-start.10 = (f32[4,32,128]{2,1,0:T(8,128)S(1)}, f32[4,32,128]{2,1,0:T(8,128)S(1)}, u32[]{:S(2)}, u32[]{:S(2)}) collective-permute-start(f32[4,32,128]{2,1,0:T(8,128)S(1)} %turn.1.own_ref), channel_id=1, source_target_pairs={{0,128},{64,192},{128,0},{192,64},{1,129},{65,193},{129,1},{193,65... | collective-permute-start | bytes 196616 | tf_op jit(solution)/shard_map/ppermute | solution.py:235
  33.3 1.2 %collective-permute-start.9 = (f32[4,32,128]{2,1,0:T(8,128)S(1)}, f32[4,32,128]{2,1,0:T(8,128)S(1)}, u32[]{:S(2)}, u32[]{:S(2)}) collective-permute-start(f32[4,32,128]{2,1,0:T(8,128)S(1)} %turn.1.own_ref), channel_id=1, source_target_pairs={{0,64},{64,0},{128,192},{192,128},{1,65},{65,1},{129,193},{193,129... | collective-permute-start | bytes 196616 | tf_op jit(solution)/shard_map/ppermute | solution.py:235
  34.5 0.0 collective-permute-done.13
  34.5 1.2 %collective-permute-done.12 = f32[4,32,128]{2,1,0:T(8,128)S(1)} collective-permute-done((f32[4,32,128]{2,1,0:T(8,128)S(1)}, f32[4,32,128]{2,1,0:T(8,128)S(1)}, u32[]{:S(2)}, u32[]{:S(2)}) %collective-permute-start.12) | collective-permute-done | bytes 65568 | tf_op jit(solution)/shard_map/ppermute | solution.py:235
  35.8 0.6 %collective-permute-start.17 = (f32[2,4,32,128]{3,2,1,0:T(8,128)S(1)}, f32[2,4,32,128]{3,2,1,0:T(8,128)S(1)}, u32[]{:S(2)}, u32[]{:S(2)}) collective-permute-start(f32[2,4,32,128]{3,2,1,0:T(8,128)S(1)} %pad_maximum_fusion.1), channel_id=1, source_target_pairs={{0,192},{64,128},{128,64},{192,0},{1,193},{65,129},{129,65},{193,1... | collective-permute-start | bytes 393224 | tf_op jit(solution)/shard_map/ppermute | solution.py:235
  36.4 2.4 %collective-permute-start.16 = (f32[2,4,32,128]{3,2,1,0:T(8,128)S(1)}, f32[2,4,32,128]{3,2,1,0:T(8,128)S(1)}, u32[]{:S(2)}, u32[]{:S(2)}) collective-permute-start(f32[2,4,32,128]{3,2,1,0:T(8,128)S(1)} %pad_maximum_fusion.1), channel_id=1, source_target_pairs={{0,128},{64,192},{128,0},{192,64},{1,129},{65,193},{129,1},{193,65... | collective-permute-start | bytes 393224 | tf_op jit(solution)/shard_map/ppermute | solution.py:235
  38.8 0.0 collective-permute-done.11
  38.8 1.2 %collective-permute-start.15 = (f32[2,4,32,128]{3,2,1,0:T(8,128)S(1)}, f32[2,4,32,128]{3,2,1,0:T(8,128)S(1)}, u32[]{:S(2)}, u32[]{:S(2)}) collective-permute-start(f32[2,4,32,128]{3,2,1,0:T(8,128)S(1)} %pad_maximum_fusion.1), channel_id=1, source_target_pairs={{0,64},{64,0},{128,192},{192,128},{1,65},{65,1},{129,193},{193,129... | collective-permute-start | bytes 393224 | tf_op jit(solution)/shard_map/ppermute | solution.py:235
  40.0 0.0 collective-permute-done.10
  40.0 0.0 collective-permute-done.9
  40.0 0.1 collective-permute-start.14
  40.2 0.7 %prepare.1 = (bf16[4,128,256]{2,1,0:T(8,128)(2,1)S(1)}, bf16[4,512,128]{2,1,0:T(8,128)(2,1)S(1)}) custom-call(s32[6]{0:T(128)S(1)} %stack.61.place, f32[4,32,128]{2,1,0:T(8,128)S(1)} %turn.1.own_ref, f32[6,4,32,128]{3,2,1,0:T(8,128)S(1)} %constant_dynamic-update-slice_fusion.block), custom_call_target="tpu_custom_call" | custom-call | tf_op jit(solution)/shard_map/prepare/pallas_call | solution.py:209
  40.8 2.6 %collective-permute-done.17.refs_3_ = f32[2,4,32,128]{3,2,1,0:T(8,128)S(1)} collective-permute-done((f32[2,4,32,128]{3,2,1,0:T(8,128)S(1)}, f32[2,4,32,128]{3,2,1,0:T(8,128)S(1)}, u32[]{:S(2)}, u32[]{:S(2)}) %collective-permute-start.17) | collective-permute-done | bytes 131104 | tf_op jit(solution)/shard_map/ppermute | solution.py:235
  43.5 0.0 collective-permute-done.16.refs_2_
  43.5 0.9 %collective-permute-done.15.refs_1_ = f32[2,4,32,128]{3,2,1,0:T(8,128)S(1)} collective-permute-done((f32[2,4,32,128]{3,2,1,0:T(8,128)S(1)}, f32[2,4,32,128]{3,2,1,0:T(8,128)S(1)}, u32[]{:S(2)}, u32[]{:S(2)}) %collective-permute-start.15) | collective-permute-done | bytes 131104 | tf_op jit(solution)/shard_map/ppermute | solution.py:235
  44.3 2.1 %collective-permute-done.14.refs_0_ = f32[4,4,32,128]{3,2,1,0:T(8,128)S(1)} collective-permute-done((f32[4,4,32,128]{3,2,1,0:T(8,128)S(1)}, f32[4,4,32,128]{3,2,1,0:T(8,128)S(1)}, u32[]{:S(2)}, u32[]{:S(2)}) %collective-permute-start.14) | collective-permute-done | bytes 262176 | tf_op jit(solution)/shard_map/ppermute | solution.py:235
  46.5 1.8 %gram.1 = (f32[2,8,32,512]{3,2,1,0:T(8,128)}, bf16[4,512,128]{2,1,0:T(8,128)(2,1)S(1)}) custom-call(s32[6]{0:T(128)S(1)} %stack.61.place, bf16[4,128,256]{2,1,0:T(8,128)(2,1)S(1)} %get-tuple-element.16.left_ref, bf16[4,512,128]{2,1,0:T(8,128)(2,1)S(1)} %get-tuple-element.17.right_in, ...), custom_call_target="tpu_custom_call", output_to_operand_aliasing={{1}: (2, {})} | custom-call | tf_op jit(solution)/shard_map/gram/pallas_call | solution.py:217
  (14 shorter events, 0.2 us)
Async XLA Ops:
  6.1 1.6 %collective-permute-start.4 = (f32[4,2,8,8,128]{4,3,2,1,0:T(8,128)S(1)}, f32[4,2,8,8,128]{4,3,2,1,0:T(8,128)S(1)}, u32[]{:S(2)}, u32[]{:S(2)}) collective-permute-start(f32[4,2,8,8,128]{4,3,2,1,0:T(8,128)S(1)} %get-tuple-element.15), channel_id=1, source_target_pairs={{0,1},{1,0},{2,3},{3,2},{4,5},{5,4},{6,7},{7,6},{8,9},{9,8},{10,11... | collective-permute-start | bytes 786440 | tf_op jit(solution)/shard_map/ppermute | solution.py:235
  6.2 7.5 %collective-permute-start = (f32[4,2,8,8,128]{4,3,2,1,0:T(8,128)S(1)}, f32[4,2,8,8,128]{4,3,2,1,0:T(8,128)S(1)}, u32[]{:S(2)}, u32[]{:S(2)}) collective-permute-start(f32[4,2,8,8,128]{4,3,2,1,0:T(8,128)S(1)} %get-tuple-element.13), channel_id=1, source_target_pairs={{0,1},{1,0},{2,3},{3,2},{4,5},{5,4},{6,7},{7,6},{8,9},{9,8},{10,11... | collective-permute-start | bytes 786440 | tf_op jit(solution)/shard_map/ppermute | solution.py:235
  7.8 7.5 %collective-permute-start.5 = (f32[2,8,8,128]{3,2,1,0:T(8,128)S(1)}, f32[2,8,8,128]{3,2,1,0:T(8,128)S(1)}, u32[]{:S(2)}, u32[]{:S(2)}) collective-permute-start(f32[2,8,8,128]{3,2,1,0:T(8,128)S(1)} %get-tuple-element.19), channel_id=1, source_target_pairs={{0,4},{4,8},{8,12},{12,0},{1,5},{5,9},{9,13},{13,1},{2,6},{6,10},{... | collective-permute-start | bytes 196616 | tf_op jit(solution)/shard_map/ppermute | solution.py:231
  9.5 7.8 %collective-permute-start.7 = (f32[2,8,8,128]{3,2,1,0:T(8,128)S(1)}, f32[2,8,8,128]{3,2,1,0:T(8,128)S(1)}, u32[]{:S(2)}, u32[]{:S(2)}) collective-permute-start(f32[2,8,8,128]{3,2,1,0:T(8,128)S(1)} %get-tuple-element.20), channel_id=1, source_target_pairs={{0,8},{4,12},{8,0},{12,4},{1,9},{5,13},{9,1},{13,5},{2,10},{6,14},... | collective-permute-start | bytes 196616 | tf_op jit(solution)/shard_map/ppermute | solution.py:231
  12.4 4.9 %collective-permute-start.6 = (f32[2,8,8,128]{3,2,1,0:T(8,128)S(1)}, f32[2,8,8,128]{3,2,1,0:T(8,128)S(1)}, u32[]{:S(2)}, u32[]{:S(2)}) collective-permute-start(f32[2,8,8,128]{3,2,1,0:T(8,128)S(1)} %get-tuple-element.21), channel_id=1, source_target_pairs={{0,12},{4,0},{8,4},{12,8},{1,13},{5,1},{9,5},{13,9},{2,14},{6,2},{... | collective-permute-start | bytes 196616 | tf_op jit(solution)/shard_map/ppermute | solution.py:231
  13.8 10.8 %collective-permute-start.1 = (f32[2,8,8,128]{3,2,1,0:T(8,128)S(1)}, f32[2,8,8,128]{3,2,1,0:T(8,128)S(1)}, u32[]{:S(2)}, u32[]{:S(2)}) collective-permute-start(f32[2,8,8,128]{3,2,1,0:T(8,128)S(1)} %get-tuple-element.22), channel_id=1, source_target_pairs={{0,4},{4,8},{8,12},{12,0},{1,5},{5,9},{9,13},{13,1},{2,6},{6,10},{... | collective-permute-start | bytes 196616 | tf_op jit(solution)/shard_map/ppermute | solution.py:231
  14.5 10.1 %collective-permute-start.3 = (f32[2,8,8,128]{3,2,1,0:T(8,128)S(1)}, f32[2,8,8,128]{3,2,1,0:T(8,128)S(1)}, u32[]{:S(2)}, u32[]{:S(2)}) collective-permute-start(f32[2,8,8,128]{3,2,1,0:T(8,128)S(1)} %get-tuple-element.23), channel_id=1, source_target_pairs={{0,8},{4,12},{8,0},{12,4},{1,9},{5,13},{9,1},{13,5},{2,10},{6,14},... | collective-permute-start | bytes 196616 | tf_op jit(solution)/shard_map/ppermute | solution.py:231
  15.3 9.3 %collective-permute-start.2 = (f32[2,8,8,128]{3,2,1,0:T(8,128)S(1)}, f32[2,8,8,128]{3,2,1,0:T(8,128)S(1)}, u32[]{:S(2)}, u32[]{:S(2)}) collective-permute-start(f32[2,8,8,128]{3,2,1,0:T(8,128)S(1)} %get-tuple-element.24), channel_id=1, source_target_pairs={{0,12},{4,0},{8,4},{12,8},{1,13},{5,1},{9,5},{13,9},{2,14},{6,2},{... | collective-permute-start | bytes 196616 | tf_op jit(solution)/shard_map/ppermute | solution.py:231
  17.3 9.6 %collective-permute-start.8 = (f32[2,8,8,128]{3,2,1,0:T(8,128)S(1)}, f32[2,8,8,128]{3,2,1,0:T(8,128)S(1)}, u32[]{:S(2)}, u32[]{:S(2)}) collective-permute-start(f32[2,8,8,128]{3,2,1,0:T(8,128)S(1)} %fusion.2), channel_id=1, source_target_pairs={{0,2},{2,0},{1,3},{3,1},{4,6},{6,4},{5,7},{7,5},{8,10},{10,8},{9,1... | collective-permute-start | bytes 196616 | tf_op jit(solution)/shard_map/ppermute | solution.py:235
  27.1 7.5 %collective-permute-start.13 = (f32[4,32,128]{2,1,0:T(8,128)S(1)}, f32[4,32,128]{2,1,0:T(8,128)S(1)}, u32[]{:S(2)}, u32[]{:S(2)}) collective-permute-start(f32[4,32,128]{2,1,0:T(8,128)S(1)} %turn.1.own_ref), channel_id=1, source_target_pairs={{0,48},{16,32},{32,16},{48,0},{1,49},{17,33},{33,17},{49,1},{2,50}... | collective-permute-start | bytes 196616 | tf_op jit(solution)/shard_map/ppermute | solution.py:235
  30.4 5.4 %collective-permute-start.12 = (f32[4,32,128]{2,1,0:T(8,128)S(1)}, f32[4,32,128]{2,1,0:T(8,128)S(1)}, u32[]{:S(2)}, u32[]{:S(2)}) collective-permute-start(f32[4,32,128]{2,1,0:T(8,128)S(1)} %turn.1.own_ref), channel_id=1, source_target_pairs={{0,32},{16,48},{32,0},{48,16},{1,33},{17,49},{33,1},{49,17},{2,34}... | collective-permute-start | bytes 196616 | tf_op jit(solution)/shard_map/ppermute | solution.py:235
  30.4 8.4 %collective-permute-start.11 = (f32[4,32,128]{2,1,0:T(8,128)S(1)}, f32[4,32,128]{2,1,0:T(8,128)S(1)}, u32[]{:S(2)}, u32[]{:S(2)}) collective-permute-start(f32[4,32,128]{2,1,0:T(8,128)S(1)} %turn.1.own_ref), channel_id=1, source_target_pairs={{0,192},{64,128},{128,64},{192,0},{1,193},{65,129},{129,65},{193,1... | collective-permute-start | bytes 196616 | tf_op jit(solution)/shard_map/ppermute | solution.py:235
  30.9 9.1 %collective-permute-start.10 = (f32[4,32,128]{2,1,0:T(8,128)S(1)}, f32[4,32,128]{2,1,0:T(8,128)S(1)}, u32[]{:S(2)}, u32[]{:S(2)}) collective-permute-start(f32[4,32,128]{2,1,0:T(8,128)S(1)} %turn.1.own_ref), channel_id=1, source_target_pairs={{0,128},{64,192},{128,0},{192,64},{1,129},{65,193},{129,1},{193,65... | collective-permute-start | bytes 196616 | tf_op jit(solution)/shard_map/ppermute | solution.py:235
  33.3 6.7 %collective-permute-start.9 = (f32[4,32,128]{2,1,0:T(8,128)S(1)}, f32[4,32,128]{2,1,0:T(8,128)S(1)}, u32[]{:S(2)}, u32[]{:S(2)}) collective-permute-start(f32[4,32,128]{2,1,0:T(8,128)S(1)} %turn.1.own_ref), channel_id=1, source_target_pairs={{0,64},{64,0},{128,192},{192,128},{1,65},{65,1},{129,193},{193,129... | collective-permute-start | bytes 196616 | tf_op jit(solution)/shard_map/ppermute | solution.py:235
  35.8 7.7 %collective-permute-start.17 = (f32[2,4,32,128]{3,2,1,0:T(8,128)S(1)}, f32[2,4,32,128]{3,2,1,0:T(8,128)S(1)}, u32[]{:S(2)}, u32[]{:S(2)}) collective-permute-start(f32[2,4,32,128]{3,2,1,0:T(8,128)S(1)} %pad_maximum_fusion.1), channel_id=1, source_target_pairs={{0,192},{64,128},{128,64},{192,0},{1,193},{65,129},{129,65},{193,1... | collective-permute-start | bytes 393224 | tf_op jit(solution)/shard_map/ppermute | solution.py:235
  36.4 7.1 %collective-permute-start.16 = (f32[2,4,32,128]{3,2,1,0:T(8,128)S(1)}, f32[2,4,32,128]{3,2,1,0:T(8,128)S(1)}, u32[]{:S(2)}, u32[]{:S(2)}) collective-permute-start(f32[2,4,32,128]{3,2,1,0:T(8,128)S(1)} %pad_maximum_fusion.1), channel_id=1, source_target_pairs={{0,128},{64,192},{128,0},{192,64},{1,129},{65,193},{129,1},{193,65... | collective-permute-start | bytes 393224 | tf_op jit(solution)/shard_map/ppermute | solution.py:235
  38.8 5.5 %collective-permute-start.15 = (f32[2,4,32,128]{3,2,1,0:T(8,128)S(1)}, f32[2,4,32,128]{3,2,1,0:T(8,128)S(1)}, u32[]{:S(2)}, u32[]{:S(2)}) collective-permute-start(f32[2,4,32,128]{3,2,1,0:T(8,128)S(1)} %pad_maximum_fusion.1), channel_id=1, source_target_pairs={{0,64},{64,0},{128,192},{192,128},{1,65},{65,1},{129,193},{193,129... | collective-permute-start | bytes 393224 | tf_op jit(solution)/shard_map/ppermute | solution.py:235
  40.0 6.5 %collective-permute-start.14 = (f32[4,4,32,128]{3,2,1,0:T(8,128)S(1)}, f32[4,4,32,128]{3,2,1,0:T(8,128)S(1)}, u32[]{:S(2)}, u32[]{:S(2)}) collective-permute-start(f32[4,4,32,128]{3,2,1,0:T(8,128)S(1)} %pad_maximum_fusion), channel_id=1, source_target_pairs={{0,16},{16,0},{32,48},{48,32},{1,17},{17,1},{33,49},{49,33},{2,18}... | collective-permute-start | bytes 786440 | tf_op jit(solution)/shard_map/ppermute | solution.py:235
